TPU v7x, 128 devices: a whole 4x4x4 slice. The times are simulated.
128 devices in a mesh: pipe: 8 (over x_lo, z), ctx: 16 (over y, x_hi, core).
Axes of the slice: x: 4 (x_hi: 2, x_lo: 2; x = x_hi * 2 + x_lo), y: 4, z: 4, core: 2. Of those that a mesh axis runs over, the one named last changes fastest.
Arguments:
- queries: bfloat16 [8, 6144, 4096], P('pipe', 'ctx'), may hold values from -1.796875 to 1.796875
- key_rows: bfloat16 [8, 6144, 4096], P('pipe', 'ctx'), may hold values from -1.796875 to 1.796875
- value_rows: bfloat16 [8, 6144, 4096], P('pipe', 'ctx'), may hold values from -6 to 6
- next_grads: bfloat16 [8, 6144, 4096], P('pipe', 'ctx'), may hold values from -0.29882812 to 0.29882812
- log_decay: float32 [8, 32, 6144], P('pipe', None, 'ctx'), may hold values from -1.5 to 0, as said below
- doc_ids: int32 [8, 6144], P('pipe', 'ctx'), may hold values from 0 to 3, never falling along the last dimension, each value on 1 to 3072 neighbouring positions
- prefix_states: float32 [8, 16, 32, 128, 128], P('pipe', 'ctx'), may hold values from -24 to 24
Outputs:
- grad_q: bfloat16 [8, 6144, 4096], P('pipe', 'ctx')
- grad_k: bfloat16 [8, 6144, 4096], P('pipe', 'ctx')
- grad_v: bfloat16 [8, 6144, 4096], P('pipe', 'ctx')
Inputs may be any that keep to these rules, and one draw needn't show every extreme that they name: `doc_ids`: in each section ids never fall along the sequence; each of the 4 documents holds 1 to 3072 tokens, one exactly 3072. `log_decay`: every entry is negative.
All inputs are finite; a program needn't handle non-finite values.
Results may differ from a plain program's by a relative error of at most 0.0053.
Values may be sent and summed in bfloat16 or wider, within the bound.
No kernel may reach another device: no remote copies, remote signals or barrier semaphores. Data moves between devices by JAX's collectives and lax.ppermute only.
A program may use at most 192 MiB of HBM per device.

v0:
```python
import jax
import jax.numpy as jnp
from jax import lax
from jax.sharding import PartitionSpec as P


def passed_along(value, axis, steps):
    count = lax.axis_size(axis)
    pairs = [(source, (source + steps) % count) for source in range(count)]
    return lax.ppermute(value, axis, pairs)


def shifted(block, axis, distance):
    devices = range(lax.axis_size(axis))
    route = [(i - distance, i) for i in devices if i - distance in devices]
    return lax.ppermute(block, axis, route)


def carried_in(part, axis, combine, identity):
    count = lax.axis_size(axis)
    place = lax.axis_index(axis)
    ahead = count - 1 - place
    gathered = jax.tree.map(lambda a: lax.all_gather(a, axis), part)
    state = jax.tree.map(lambda a, e: jnp.zeros_like(a) + jnp.asarray(e, a.dtype), part, identity)

    def one(turn, state):
        source = count - 1 - turn
        return combine(
            state, jax.tree.map(lambda a: lax.dynamic_index_in_dim(a, source, 0, False), gathered)
        )

    return lax.fori_loop(0, ahead, one, state)


def local_block(
    queries, key_rows, value_rows, grad_rows, log_decay, doc_ids, prefix_state, prior_last
):
    head_count = log_decay.shape[0]
    length = queries.shape[0]
    head_dim = queries.shape[1] // head_count
    query_heads = queries.reshape(length, head_count, head_dim)
    key_heads = key_rows.reshape(length, head_count, head_dim)
    value_heads = value_rows.reshape(length, head_count, head_dim)
    grad_heads = grad_rows.reshape(length, head_count, head_dim)
    running = jnp.cumsum(log_decay, axis=1)
    block_total = running[:, -1]
    position = lax.iota(jnp.int32, length)
    same_doc = (doc_ids[:, None] == doc_ids[None, :]) & (position[None, :] <= position[:, None])
    spread = running[:, :, None] - running[:, None, :]
    weight = jnp.where(same_doc[None], jnp.exp(jnp.where(same_doc[None], spread, 0.0)), 0.0)
    scores = jnp.einsum("ihd,jhd->hij", query_heads, key_heads, preferred_element_type=jnp.float32)
    attention = (weight * scores).astype(jnp.bfloat16)
    grad_dots = jnp.einsum(
        "ihd,jhd->hij", grad_heads, value_heads, preferred_element_type=jnp.float32
    )
    grad_mix = (weight * grad_dots).astype(jnp.bfloat16)
    continues = prior_last == doc_ids[0] + 1
    head_mask = jnp.where((doc_ids == doc_ids[0]) & continues, 1.0, 0.0)
    head_weight = jnp.exp(running).T * head_mask[:, None]
    weighted = (head_weight[:, :, None] * grad_heads).astype(jnp.bfloat16)
    head_state = jnp.einsum(
        "ihd,ihe->hde", query_heads, weighted, preferred_element_type=jnp.float32
    )
    carry_link = jnp.where((doc_ids[0] == doc_ids[-1]) & continues, jnp.exp(block_total), 0.0)
    grad_prefix = (
        jnp.einsum(
            "hde,ihe->ihd",
            prefix_state.astype(jnp.bfloat16),
            grad_heads,
            preferred_element_type=jnp.float32,
        )
        * head_weight[:, :, None]
    )
    grad_query = (
        jnp.einsum("hij,jhd->ihd", grad_mix, key_heads, preferred_element_type=jnp.float32)
        + grad_prefix
    )
    key_inner = jnp.einsum(
        "hij,ihd->jhd", grad_mix, query_heads, preferred_element_type=jnp.float32
    )
    value_inner = jnp.einsum(
        "hij,ihd->jhd", attention, grad_heads, preferred_element_type=jnp.float32
    )
    tail_mask = (doc_ids == doc_ids[-1])[None, :]
    tail_weight = jnp.where(
        tail_mask, jnp.exp(jnp.where(tail_mask, block_total[:, None] - running, 0.0)), 0.0
    ).T
    grad_query = grad_query.astype(jnp.bfloat16).reshape(length, -1)
    return (grad_query, key_inner, value_inner, head_state, carry_link, tail_weight)


def on_device(queries, key_rows, value_rows, next_grads, log_decay, doc_ids, prefix_states):
    out_grads = passed_along(next_grads, "pipe", -1)
    doc_row = doc_ids[0]
    prior_last = shifted(doc_row[-1:] + 1, "ctx", 1)
    grad_query, key_inner, value_inner, head_state, carry_link, tail_weight = local_block(
        queries[0],
        key_rows[0],
        value_rows[0],
        out_grads[0],
        log_decay[0],
        doc_row,
        prefix_states[0, 0],
        prior_last[0],
    )

    def combine(earlier_part, later_part):
        return (
            later_part[0] * earlier_part[0],
            later_part[1] + later_part[0][:, None, None] * earlier_part[1],
        )

    identity = (jnp.ones_like(carry_link), jnp.zeros_like(head_state))
    suffix = carried_in((carry_link, head_state), "ctx", combine, identity)[1]
    length = key_rows.shape[1]
    head_count = suffix.shape[0]
    head_dim = suffix.shape[1]
    key_heads = key_rows[0].reshape(length, head_count, head_dim)
    value_heads = value_rows[0].reshape(length, head_count, head_dim)
    suffix_low = suffix.astype(jnp.bfloat16)
    grad_key = (
        key_inner
        + jnp.einsum("hde,jhe->jhd", suffix_low, value_heads, preferred_element_type=jnp.float32)
        * tail_weight[:, :, None]
    )
    grad_value = (
        value_inner
        + jnp.einsum("hde,jhd->jhe", suffix_low, key_heads, preferred_element_type=jnp.float32)
        * tail_weight[:, :, None]
    )
    grad_key = grad_key.astype(jnp.bfloat16).reshape(length, -1)
    grad_value = grad_value.astype(jnp.bfloat16).reshape(length, -1)
    return (grad_query[None], grad_key[None], grad_value[None])


def solution(mesh):
    return jax.shard_map(
        on_device,
        mesh=mesh,
        in_specs=(
            P("pipe", "ctx", None),
            P("pipe", "ctx", None),
            P("pipe", "ctx", None),
            P("pipe", "ctx", None),
            P("pipe", None, "ctx"),
            P("pipe", "ctx"),
            P("pipe", "ctx", None, None, None),
        ),
        out_specs=(P("pipe", "ctx", None), P("pipe", "ctx", None), P("pipe", "ctx", None)),
        check_vma=False,
    )
```

profile of v0, /device:TPU:0, one launch (start us, length us, event | category | flops | bytes accessed | tf_op | source)
XLA Modules:
  0.0 371.8 jit_solution(6977419638870837130)
XLA Ops:
  7.2 0.0 copy-start.6
  7.2 0.0 copy-start.5
  7.2 0.0 all-gather.4.cloned.1.call-start
  7.2 4.6 %copy.65 = bf16[1,384,4096]{1,2,0:T(8,128)(2,1)} copy(bf16[1,384,4096]{2,1,0:T(8,128)(2,1)} %param.12) | data formatting | bytes 6291456 | tf_op args[3]
  11.9 5.0 %collective-permute-start = (bf16[1,384,4096]{1,2,0:T(8,128)(2,1)}, bf16[1,384,4096]{1,2,0:T(8,128)(2,1)}, u32[]{:S(2)}, u32[]{:S(2)}) collective-permute-start(bf16[1,384,4096]{1,2,0:T(8,128)(2,1)} %copy.65), channel_id=1, source_target_pairs={{0,112},{16,0},{32,16},{48,32},{64,48},{80,64},{96,80},{112,96},{1... | collective-permute-start | bytes 9437192 | tf_op jit(solution)/shard_map/ppermute | solution.py:10
  16.9 0.0 copy-done.6
  16.9 0.6 fusion.41
  18.2 2.4 collective-permute-start.1
  22.5 0.0 copy-done.5
  22.6 0.9 reduce-window.6
  23.4 0.2 slice_reduce_fusion
  23.7 2.7 copy.87
  26.4 0.0 copy-start.3
  26.4 0.7 compare_reduce_fusion
  27.1 0.1 copy_bitcast_fusion
  27.7 0.2 slice_reduce_fusion.1
  27.9 0.7 and_select_fusion
  28.6 0.1 select_bitcast_fusion
  28.7 55.9 %collective-permute-done = bf16[1,384,4096]{1,2,0:T(8,128)(2,1)} collective-permute-done((bf16[1,384,4096]{1,2,0:T(8,128)(2,1)}, bf16[1,384,4096]{1,2,0:T(8,128)(2,1)}, u32[]{:S(2)}, u32[]{:S(2)}) %collective-permute-start) | collective-permute-done | bytes 3145760 | tf_op jit(solution)/shard_map/ppermute | solution.py:10
  84.6 6.3 %fusion.32 = f32[32,128,128]{1,2,0:T(8,128)} fusion(bf16[384,32,128]{2,1,0:T(8,128)(2,1)S(1)} %bitcast.81, bf16[384,32,128]{0,2,1:T(8,128)(2,1)} %bitcast.2, f32[384,32]{0,1:T(8,128)S(1)} %get-tuple-element.128), kind=kOutput, calls=%fused_computation.34 | convolution fusion | flops 407371776 | bytes 8437760 | tf_op jit(solution)/shard_map/ihd,ihe->hde/dot_general | solution.py:61
  90.9 0.0 copy-done.3
  90.9 2.9 copy.72
  93.8 0.0 all-gather.4.cloned.1.call-update
  93.9 0.0 copy-start.4
  93.9 4.6 %copy.85 = bf16[48,8,32,128]{3,2,1,0:T(8,128)(2,1)} copy(bf16[48,8,32,128]{3,1,2,0:T(8,128)(2,1)} %bitcast.90) | data formatting | bytes 6291456
  98.4 0.0 copy-done.4
  98.4 0.8 copy.86
  99.3 0.7 dynamic-slice
  100.6 0.1 fusion.37
  100.8 0.2 dynamic-update-slice
  101.0 40.9 %all-reduce = f32[512]{0:T(512)S(1)} all-reduce(f32[512]{0:T(512)S(1)} %dynamic-update-slice), channel_id=3, replica_groups=mesh['pipe'=8,'ctx'=16] {'ctx'}, use_global_device_ids=true, to_apply=%add | all-reduce | flops 512 | bytes 4096
  141.9 0.1 reshape.122
  142.0 15.8 %multiply_convert_fusion.1 = bf16[32,384,384]{2,1,0:T(8,128)(2,1)} fusion(f32[32,384]{1,0:T(8,128)S(1)} %copy_bitcast_fusion, pred[384,384]{1,0:T(8,128)(4,1)S(1)} %fusion.37, bf16[384,32,128]{0,2,1:T(8,128)(2,1)} %bitcast.2, bf16[384,32,128]{2,1,0:T(8,128)(2,1)} %bitcast.85), kind=kOutput, calls=%fused_computation.3 | convolution fusion | flops 1231552512 | bytes 15925248 | tf_op jit(solution)/shard_map/ihd,jhd->hij/dot_general | solution.py:53
  157.9 10.5 %fusion.18 = f32[32,384,128]{1,2,0:T(8,128)} fusion(bf16[32,384,384]{2,1,0:T(8,128)(2,1)} %multiply_convert_fusion.1, bf16[384,32,128]{2,1,0:T(8,128)(2,1)S(1)} %bitcast.78), kind=kOutput, calls=%fused_computation.26 | convolution fusion | flops 1207959552 | bytes 18874368 | tf_op jit(solution)/shard_map/hij,jhd->ihd/dot_general | solution.py:75
  168.3 5.4 %fusion.10 = bf16[384,32,128]{0,2,1:T(8,128)(2,1)S(1)} fusion(f32[32,384,128]{1,2,0:T(8,128)} %fusion.18, f32[384,32]{0,1:T(8,128)S(1)} %get-tuple-element.128, bf16[384,32,128]{0,2,1:T(8,128)(2,1)} %bitcast.2, f32[1,1,32,128,128]{4,3,2,1,0:T(8,128)} %param.15), kind=kOutput, calls=%fused_computation.18 | convolution fusion | flops 407896064 | bytes 14729216 | tf_op jit(solution)/shard_map/hde,ihe->ihd/dot_general | solution.py:66
  173.7 2.9 copy.78
  176.5 109.1 %all-gather.4.cloned.1.call-done = f32[512,128,128]{2,1,0:T(8,128)} async-done(((f32[32,128,128]{2,1,0:T(8,128)}), f32[512,128,128]{2,1,0:T(8,128)}) %all-gather.4.cloned.1.call-update) | async-done | bytes 33554448 | tf_op jit(solution)/shard_map/all_gather | solution.py:23
  285.7 0.2 broadcast_in_dim.68
  285.9 30.6 %while.14 = (s32[]{:T(128)}, f32[32,128,128]{2,1,0:T(8,128)S(1)}, s32[]{:T(128)}, f32[16,32,128,128]{3,2,1,0:T(8,128)}, f32[16,32]{1,0:T(8,128)S(1)}, /*index=5*/s32[]{:T(128)}, s32[]{:T(128)}, s32[]{:T(128)}, s32[]{:T(128)}) while((s32[]{:T(128)}, f32[32,128,128]{2,1,0:T(8,128)S(1)}, s32[]{:T(128)}, f32[16,32,128,128]{3,2,1,0:T(8,128)}, ...), condition=%wide.region_3.4_spmd, body=%wide.region_2.3_spmd.sunk | while | flops 1048582 | bytes 6291987 | solution.py:32
  285.9 2.0 bitcast_add_fusion.2
  288.0 2.0 bitcast_add_fusion.2
  290.0 2.0 bitcast_add_fusion.2
  292.0 2.0 bitcast_add_fusion.2
  294.0 2.0 bitcast_add_fusion.2
  296.1 2.0 bitcast_add_fusion.2
  298.1 2.0 bitcast_add_fusion.2
  300.1 2.0 bitcast_add_fusion.2
  302.1 2.0 bitcast_add_fusion.2
  304.2 2.0 bitcast_add_fusion.2
  306.2 2.0 bitcast_add_fusion.2
  308.2 2.0 bitcast_add_fusion.2
  310.2 2.0 bitcast_add_fusion.2
  312.3 2.0 bitcast_add_fusion.2
  314.3 2.0 bitcast_add_fusion.2
  316.5 0.0 slice-start
  316.5 0.0 slice-start.1
  316.5 7.8 %fusion.15 = f32[32,128,384]{2,1,0:T(8,128)} fusion(bf16[384,32,128]{2,1,0:T(8,128)(2,1)} %bitcast.86, f32[32,128,128]{2,1,0:T(8,128)S(1)} %get-tuple-element.87), kind=kOutput, calls=%fused_computation.23 | convolution fusion | flops 403177472 | bytes 11534336 | tf_op jit(solution)/shard_map/hde,jhe->jhd/dot_general | solution.py:123
  324.4 0.0 copy-done.1
  324.4 6.5 %fusion.20 = f32[32,128,384]{2,1,0:T(8,128)} fusion(bf16[384,32,128]{2,1,0:T(8,128)(2,1)S(1)} %bitcast.79, f32[32,128,128]{2,1,0:T(8,128)S(1)} %get-tuple-element.87), kind=kOutput, calls=%fused_computation.28 | convolution fusion | flops 403177472 | bytes 11534336 | tf_op jit(solution)/shard_map/hde,jhd->jhe/dot_general | solution.py:128
  330.9 0.0 slice-done.1
  330.9 9.8 %fusion.8 = bf16[384,32,128]{0,2,1:T(8,128)(2,1)} fusion(f32[32,128,384]{2,1,0:T(8,128)} %fusion.15, f32[384,32]{0,1:T(8,128)S(1)} %get-tuple-element.127, bf16[32,384,384]{2,1,0:T(8,128)(2,1)S(1)} %bitcast.77, bf16[384,32,128]{2,1,0:T(8,128)(2,1)} %bitcast.82), kind=kOutput, calls=%fused_computation.15 | convolution fusion | flops 1212678144 | bytes 22069248 | tf_op jit(solution)/shard_map/hij,ihd->jhd/dot_general | solution.py:78
  340.7 4.8 %copy.79 = bf16[1,384,4096]{2,1,0:T(8,128)(2,1)} copy(bf16[1,384,4096]{1,2,0:T(8,128)(2,1)} %bitcast.84) | data formatting | bytes 6291456
  345.5 14.8 %fusion.6 = bf16[384,32,128]{0,2,1:T(8,128)(2,1)} fusion(f32[32,128,384]{2,1,0:T(8,128)} %fusion.20, f32[384,32]{0,1:T(8,128)S(1)} %get-tuple-element.127, bf16[384,32,128]{0,2,1:T(8,128)(2,1)} %bitcast.2, f32[32,384]{1,0:T(8,128)S(1)} %copy_bitcast_fusion, pred[384,384]{1,0:T(8,128)(4,1)S(1)} %fusion.37, bf16[384,32,128]{2,1,0:T(8,128)(2,1)S(1)} %bitcast.80, ...), kind=kOutput, calls=%fused_computation.12 | convolution fusion | flops 2444230656 | bytes 19120128 | tf_op jit(solution)/shard_map/hij,ihd->jhd/dot_general | solution.py:81
  360.4 4.6 %copy.80 = bf16[1,384,4096]{2,1,0:T(8,128)(2,1)} copy(bf16[1,384,4096]{1,2,0:T(8,128)(2,1)} %bitcast.92) | data formatting | bytes 6291456
  (32 shorter events, 0.3 us)
Async XLA Ops:
  7.2 9.8 %copy-start.6 = (s32[1,384]{1,0:T(1,128)S(1)}, s32[1,384]{1,0:T(1,128)}, u32[]{:S(2)}) copy-start(s32[1,384]{1,0:T(1,128)} %param.14) | copy-start | bytes 4612
  7.2 15.3 %copy-start.5 = (f32[1,32,384]{2,1,0:T(8,128)S(1)}, f32[1,32,384]{2,1,0:T(8,128)}, u32[]{:S(2)}) copy-start(f32[1,32,384]{2,1,0:T(8,128)} %param.13) | copy-start | bytes 147460
  7.2 278.5 %all-gather.4.cloned.1.call-start = ((), (), s32[]{:S(2)}) async-start(), calls=%async_computation | async-start | bytes 35651584 | tf_op jit(solution)/shard_map/all_gather | solution.py:23
  11.9 72.7 %collective-permute-start = (bf16[1,384,4096]{1,2,0:T(8,128)(2,1)}, bf16[1,384,4096]{1,2,0:T(8,128)(2,1)}, u32[]{:S(2)}, u32[]{:S(2)}) collective-permute-start(bf16[1,384,4096]{1,2,0:T(8,128)(2,1)} %copy.65), channel_id=1, source_target_pairs={{0,112},{16,0},{32,16},{48,32},{64,48},{80,64},{96,80},{112,96},{1... | collective-permute-start | bytes 9437192 | tf_op jit(solution)/shard_map/ppermute | solution.py:10
  18.2 9.0 %collective-permute-start.1 = (s32[1]{0:T(128)}, s32[1]{0:T(128)}, u32[]{:S(2)}, u32[]{:S(2)}) collective-permute-start(s32[1]{0:T(128)} %bitcast.7), channel_id=1, source_target_pairs={{0,1},{1,2},{2,3},{3,4},{4,5},{5,6},{6,7},{7,8},{8,9},{9,10},{10,1... | collective-permute-start | bytes 20 | tf_op jit(solution)/shard_map/ppermute | solution.py:16
  26.4 64.6 %copy-start.3 = (bf16[48,8,32,128]{3,2,1,0:T(8,128)(2,1)}, bf16[48,8,32,128]{3,2,1,0:T(8,128)(2,1)S(1)}, u32[]{:S(2)}) copy-start(bf16[48,8,32,128]{3,2,1,0:T(8,128)(2,1)S(1)} %copy.87) | copy-start | bytes 9437188
  93.9 4.6 %copy-start.4 = (bf16[1,384,4096]{2,1,0:T(8,128)(2,1)S(1)}, bf16[1,384,4096]{2,1,0:T(8,128)(2,1)}, u32[]{:S(2)}) copy-start(bf16[1,384,4096]{2,1,0:T(8,128)(2,1)} %param.10) | copy-start | bytes 9437188
  98.4 0.8 copy-start.7
  99.3 58.6 %copy-start = (bf16[48,8,32,128]{3,2,1,0:T(8,128)(2,1)}, bf16[48,8,32,128]{3,2,1,0:T(8,128)(2,1)S(1)}, u32[]{:S(2)}) copy-start(bf16[48,8,32,128]{3,2,1,0:T(8,128)(2,1)S(1)} %copy.86) | copy-start | bytes 9437188
  316.5 7.9 %copy-start.1 = (bf16[48,8,32,128]{3,2,1,0:T(8,128)(2,1)S(1)}, bf16[48,8,32,128]{3,2,1,0:T(8,128)(2,1)}, u32[]{:S(2)}) copy-start(bf16[48,8,32,128]{3,2,1,0:T(8,128)(2,1)} %copy-done) | copy-start | bytes 9437188
  316.5 14.3 %slice-start = ((s8[9437184]{0:T(1024)(128)(4,1)}), s8[4194304]{0:T(1024)(128)(4,1)S(1)}, s32[]{:S(2)}) async-start(s8[9437184]{0:T(1024)(128)(4,1)} %bitcast.76), calls=%async_computation.1 | async-start | bytes 8388608
  316.5 14.3 %slice-start.1 = ((s8[9437184]{0:T(1024)(128)(4,1)}), s8[4194304]{0:T(1024)(128)(4,1)S(1)}, s32[]{:S(2)}) async-start(s8[9437184]{0:T(1024)(128)(4,1)} %bitcast.76), calls=%async_computation.2 | async-start | bytes 8388608
  324.4 6.5 %slice-start.2 = ((s8[9437184]{0:T(1024)(128)(4,1)}), s8[1048576]{0:T(1024)(128)(4,1)S(1)}, s32[]{:S(2)}) async-start(s8[9437184]{0:T(1024)(128)(4,1)} %bitcast.76), calls=%async_computation.3 | async-start | bytes 2097152
  340.7 4.8 %copy-start.2 = (bf16[48,8,32,128]{3,2,1,0:T(8,128)(2,1)S(1)}, bf16[48,8,32,128]{3,2,1,0:T(8,128)(2,1)}, u32[]{:S(2)}) copy-start(bf16[48,8,32,128]{3,2,1,0:T(8,128)(2,1)} %copy-done) | copy-start | bytes 9437188
Sparse Core Ops, SparseCore 0:
  94.0 191.6 all-gather.3
where the time goes:
time: 373 us; the launch traced here: 372 us
  waiting for transfers between devices  165 us (44%)
  matrix products  77 us (21%)
  blocking collectives  40.9 us (11%)
  other arithmetic  32.4 us (9%)
  local copies, waits for them, and re-layouts  30.1 us (8%)
  between operations  18.1 us (5%)
  starting transfers between devices  7.49 us (2%)
    all_gather x1, waiting for transfers between devices, carried_in(): gathered = jax.tree.map(lambda a: lax.all_gather(a, axis), part)  109 us
    ppermute x1, waiting for transfers between devices, passed_along(): return lax.ppermute(value, axis, pairs)  55.9 us
    unnamed x1, blocking collectives  40.9 us
    add x15, other arithmetic, combine(): later_part[1] + later_part[0][:, None, None] * earlier_part[1]  29.6 us
    unnamed x32, local copies, waits for them, and re-layouts  26 us
    dot_general x1, matrix products, local_block(): jnp.einsum('ihd,jhd->hij', grad_heads, value_heads, preferred_element_typ...  15.8 us
    dot_general x1, matrix products, local_block(): jnp.einsum('hij,ihd->jhd', attention, grad_heads, preferred_element_type=...  14.8 us
    dot_general x1, matrix products, local_block(): jnp.einsum('hij,jhd->ihd', grad_mix, key_heads, preferred_element_type=jn...  10.5 us
  transfers between devices with their start and end apart: 3, of which 2 were waited for; matrix products, arithmetic and copies ran while one was open for 13% of the time, Pallas kernels for 0%

commit v1 on v0

v1 whole, which is shorter than its diff:
```python
import functools

import jax
import jax.numpy as jnp
from jax import lax
from jax.experimental import pallas as pl
from jax.experimental.pallas import tpu as pltpu
from jax.sharding import PartitionSpec as P

D = 128
GROUPS = ((12, 12), (4, 4))
CHUNKS = sum(GROUPS, ())
PAIR = 2
PACK = 8
VMEM_BYTES = 36 << 20
NT = (((1,), (1,)), ((), ()))
NN = (((1,), (0,)), ((), ()))
TN = (((0,), (0,)), ((), ()))


def dot(a, b, dims):
    return lax.dot_general(a, b, dims, preferred_element_type=jnp.float32)


def lane(columns, n):
    return jnp.broadcast_to(columns[:, n : n + 1], (columns.shape[0], D))


def state_of(q, g, head_weight):
    weighted = (head_weight * g.astype(jnp.float32)).astype(jnp.bfloat16)
    return dot(q, weighted, TN)


def state_kernel(side_ref, q_ref, g_ref, pack_ref, state_ref):
    columns = jnp.transpose(pack_ref[0])
    for a in range(PAIR):
        cols = slice(a * D, (a + 1) * D)
        state_ref[a] = state_of(q_ref[0, :, cols], g_ref[0, :, cols], lane(columns, PAIR + a))


class Place:
    def __init__(self, start, heads, length, other_first, skipped=0):
        self.steps = heads // PAIR
        half = self.steps // 2
        base = start // PAIR
        width = PAIR * D

        def place(t, side):
            early = 1 - side[0] if other_first else side[0]
            return jnp.where(t < half, early * half + t, (1 - early) * half + t - half)

        skip = skipped // PAIR
        self.mine = pl.BlockSpec((PAIR, D, D), lambda t, s: (skip + jnp.minimum(t, half - 1), 0, 0))
        self.other = pl.BlockSpec((PAIR, D, D), lambda t, s: (skip + jnp.maximum(t - half, 0), 0, 0))
        self.state = pl.BlockSpec((PAIR, D, D), lambda t, s: (t, 0, 0))
        self.wide = pl.BlockSpec((1, length, width), lambda t, s: (0, 0, base + place(t, s)))
        self.chunk = pl.BlockSpec((1, length, width), lambda t, s: (0, 0, place(t, s)))
        self.flat = pl.BlockSpec((length, width), lambda t, s: (0, place(t, s)))
        self.square = pl.BlockSpec((1, 1, PAIR, D, D), lambda t, s: (0, 0, base + place(t, s), 0, 0))
        self.pack = pl.BlockSpec((1, PACK, length), lambda t, s: (base + place(t, s), 0, 0))
        self.whole = pl.BlockSpec((length, length), lambda t, s: (0, 0))


def call(kernel, name, place, side, args, specs, out_shapes, out_specs, kept, cost):
    args = [side, *args]
    specs = list(specs)
    aliases = {}
    for n, value in enumerate(kept):
        if value is not None:
            aliases[len(args)] = n
            args.append(value)
            specs.append(pl.BlockSpec(memory_space=pl.ANY))
    return pl.pallas_call(
        kernel,
        out_shape=tuple(out_shapes),
        grid_spec=pltpu.PrefetchScalarGridSpec(
            num_scalar_prefetch=1, grid=(place.steps,), in_specs=specs, out_specs=list(out_specs)
        ),
        input_output_aliases=aliases,
        compiler_params=pltpu.CompilerParams(vmem_limit_bytes=VMEM_BYTES),
        cost_estimate=pl.CostEstimate(**cost),
        name=name,
    )(*args)


def states_of(side, q, g, pack, start, heads):
    length = q.shape[1]
    at = Place(start, heads, length, True)
    state = jax.ShapeDtypeStruct((heads, D, D), jnp.float32)
    cost = dict(
        flops=heads * length * D * D * 2, bytes_accessed=heads * length * D * 4, transcendentals=0
    )
    return call(
        state_kernel,
        "head_states",
        at,
        side,
        (q, g, pack),
        (at.wide, at.chunk, at.pack),
        (state,),
        (at.state,),
        (),
        cost,
    )[0]


def inner_kernel(with_states, side_ref, q_ref, k_ref, v_ref, g_ref, p_ref, mask_ref, pack_ref, *rest):
    if with_states:
        gq_ref, gk_ref, gv_ref, state_ref = rest[-4:]
    else:
        gq_ref, gk_ref, gv_ref = rest[-3:]
    length = q_ref.shape[1]
    blocks = length // D
    columns = jnp.transpose(pack_ref[0])
    for a in range(PAIR):
        cols = slice(a * D, (a + 1) * D)
        q = q_ref[0, :, cols]
        k = k_ref[0, :, cols]
        v = v_ref[0, :, cols]
        g = g_ref[0, :, cols]
        head_weight = lane(columns, PAIR + a)
        if with_states:
            state_ref[a] = state_of(q, g, head_weight)
        row = pack_ref[0, a : a + 1, :]
        col = lane(columns, a)
        mixes = []
        for j in range(blocks):
            js = slice(j * D, (j + 1) * D)
            width = length - j * D
            late = slice(j * D, length)
            spread = row[:, late] - jnp.concatenate([col[js]] * (width // D), axis=1)
            weight = jnp.exp(spread + mask_ref[js, late])
            attention = (weight * dot(k[js], q[late], NT)).astype(jnp.bfloat16)
            mix = (weight * dot(v[js], g[late], NT)).astype(jnp.bfloat16)
            mixes.append(mix)
            gv_ref[js, cols] = dot(attention, g[late], NN)
            gk_ref[js, cols] = dot(mix, q[late], NN)
        prefix = dot(g, p_ref[0, 0, a].astype(jnp.bfloat16), NT) * head_weight
        for i in range(blocks):
            rows = slice(i * D, (i + 1) * D)
            parts = [mixes[j][:, (i - j) * D : (i - j + 1) * D] for j in range(i + 1)]
            mix = parts[0] if i == 0 else jnp.concatenate(parts, axis=0)
            gq = dot(mix, k[: (i + 1) * D], TN) + prefix[rows]
            gq_ref[0, rows, cols] = gq.astype(gq_ref.dtype)


def inner_of(side, q, k, v, g, prefix, mask, pack, out, start, heads, with_states):
    length = q.shape[1]
    at = Place(start, heads, length, True)
    partial = jax.ShapeDtypeStruct((length, heads * D), jnp.float32)
    state = jax.ShapeDtypeStruct((heads, D, D), jnp.float32)
    whole = jax.ShapeDtypeStruct(q.shape, jnp.bfloat16)
    cost = dict(
        flops=heads * 33 * 2 * D * D * D,
        bytes_accessed=heads * length * D * 18,
        transcendentals=heads * length * length // 2,
    )
    return call(
        functools.partial(inner_kernel, with_states),
        "inner_grads",
        at,
        side,
        (q, k, v, g, prefix, mask, pack),
        (at.wide, at.wide, at.wide, at.chunk, at.square, at.whole, at.pack),
        (whole, partial, partial) + ((state,) if with_states else ()),
        (at.wide, at.flat, at.flat) + ((at.state,) if with_states else ()),
        (out,),
        cost,
    )


def finish_kernel(side_ref, k_ref, v_ref, ki_ref, vi_ref, mine_ref, other_ref, pack_ref, *rest):
    gk_ref, gv_ref = rest[-2:]
    first = pl.program_id(0) < pl.num_programs(0) // 2
    columns = jnp.transpose(pack_ref[0])
    for a in range(PAIR):
        cols = slice(a * D, (a + 1) * D)
        weight = lane(columns, 2 * PAIR + a)
        suffix = jnp.where(first, mine_ref[a], other_ref[a])
        gk = ki_ref[:, cols] + weight * dot(v_ref[0, :, cols], suffix, NT)
        gv = vi_ref[:, cols] + weight * dot(k_ref[0, :, cols], suffix, NN)
        gk_ref[0, :, cols] = gk.astype(gk_ref.dtype)
        gv_ref[0, :, cols] = gv.astype(gv_ref.dtype)


def finish_of(side, k, v, key_inner, value_inner, mine, other, pack, outs, start, heads, skipped):
    length = k.shape[1]
    at = Place(start, heads, length, False, skipped)
    whole = jax.ShapeDtypeStruct(k.shape, jnp.bfloat16)
    cost = dict(
        flops=heads * 6 * 2 * D * D * D, bytes_accessed=heads * length * D * 16, transcendentals=0
    )
    return call(
        finish_kernel,
        "finish_grads",
        at,
        side,
        (k, v, key_inner, value_inner, mine, other, pack),
        (at.wide, at.wide, at.flat, at.flat, at.mine, at.other, at.pack),
        (whole, whole),
        (at.wide, at.wide),
        outs,
        cost,
    )


def moved(value, pairs):
    return lax.ppermute(value, "ctx", pairs)


def part_of(table, first, count):
    return lax.dynamic_slice_in_dim(table, first, count)[:, None, None]


def after(value, *others):
    return lax.optimization_barrier((value, *others))[0]


def on_device(queries, key_rows, value_rows, next_grads, log_decay, doc_ids, prefix_states):
    pipe = lax.axis_size("pipe")
    ctx = lax.axis_size("ctx")
    length = queries.shape[1]
    back = [((i + 1) % pipe, i) for i in range(pipe)]
    core_swap = [(i, i ^ 1) for i in range(ctx)]
    chip_swap = [(i, i ^ 2) for i in range(ctx)]
    row_up = [[(i, i - 4 * d) for i in range(4 * d, ctx)] for d in (1, 2)]

    starts = [sum(CHUNKS[:n]) for n in range(len(CHUNKS))]
    docs = doc_ids[0]
    prior = lax.ppermute(docs[-1:] + 1, "ctx", [(i, i + 1) for i in range(ctx - 1)])[0]
    place = lax.axis_index("ctx")
    side = place % 2
    pair = (place // 2) % 2
    even = side == 0
    near = pair == 0
    continues = prior == docs[0] + 1
    position = lax.iota(jnp.int32, length)
    upto = jnp.where(position[:, None] <= position[None, :], 1.0, 0.0)
    running = jnp.dot(log_decay[0], upto, precision=lax.Precision.HIGHEST)
    allowed = (docs[:, None] == docs[None, :]) & (position[:, None] <= position[None, :])
    mask = jnp.where(allowed, 0.0, -1e30)
    total = running[:, -1:]
    head_weight = jnp.exp(running) * jnp.where((docs == docs[0]) & continues, 1.0, 0.0)
    tail_weight = jnp.exp(total - running) * jnp.where(docs == docs[-1], 1.0, 0.0)
    pack = jnp.concatenate(
        [
            value.reshape(-1, PAIR, length)
            for value in (running, head_weight, tail_weight, jnp.zeros_like(running))
        ],
        axis=1,
    )
    link = jnp.where((docs[0] == docs[-1]) & continues, jnp.exp(running[:, -1]), 0.0)
    partner = moved(link, core_swap)
    link_even = jnp.where(even, link, partner)
    link_odd = jnp.where(even, partner, link)
    chip_link = link_even * link_odd
    near_table = jnp.stack([chip_link] + [moved(chip_link, pairs) for pairs in row_up])
    side_arr = side.astype(jnp.int32).reshape(1)

    grads = []
    for n, (start, size) in enumerate(zip(starts, CHUNKS)):
        ready = (prior, chip_link, near_table, grads[0] if n else None)[min(n, 3)]
        part = lax.slice_in_dim(after(next_grads, ready), start * D, (start + size) * D, axis=2)
        grads.append(lax.ppermute(part, "pipe", back))

    def halves(table, members):
        return jnp.concatenate([part_of(table, starts[n] + side * (CHUNKS[n] // 2), CHUNKS[n] // 2) for n in members])

    held = []
    out = None
    members = []
    for group in GROUPS:
        begin = members[-1] + 1 if members else 0
        members = list(range(begin, begin + len(group)))
        inner = {}
        states = []
        late = None
        for n in members:
            start, size, grad = starts[n], CHUNKS[n], grads[n]
            if out is not None:
                grad = after(grad, out)
            inputs = (prefix_states, mask, pack, out, start, size)
            if n == len(CHUNKS) - 1:
                state = states_of(side_arr, queries, grad, pack, start, size)
                late = (n, grad, inputs)
            else:
                out, *inner[n], state = inner_of(side_arr, queries, key_rows, value_rows, grad, *inputs, True)
            states.append(state)
        other = jnp.concatenate([state[: state.shape[0] // 2] for state in states])
        mine = jnp.concatenate([state[state.shape[0] // 2 :] for state in states])
        came = moved(other, core_swap)
        even_state = jnp.where(even, mine, came)
        odd_state = jnp.where(even, came, mine)
        state = even_state + halves(link_even, members) * odd_state
        low = state.astype(jnp.bfloat16)
        later = [moved(low, pairs) for pairs in row_up]
        if late is not None:
            n, grad, inputs = late
            out, *inner[n] = inner_of(side_arr, queries, key_rows, value_rows, after(grad, low), *inputs, False)
        held.append((members, odd_state, state, later, inner))

    beside = after(moved(near_table, chip_swap), held[-1][2])
    near_rows = jnp.where(near, near_table, beside)
    far_rows = jnp.where(near, beside, near_table)
    far_link, next_near, next_far, last_near = far_rows[0], near_rows[1], far_rows[1], near_rows[2]
    own_coef = [
        jnp.where(near, far_link, next_near),
        jnp.where(near, far_link * next_near * next_far, next_near * next_far * last_near),
    ]
    sent_coef = jnp.where(near, next_near * next_far, far_link * next_near)
    outs = (None, None)
    for members, odd_state, state, later, inner in held:
        if members[-1] < len(CHUNKS) - 1:
            state = after(state, grads[-1])
        later = [value.astype(jnp.float32) for value in later]
        near_coef, far_coef = (halves(table, members) for table in own_coef)
        coef = halves(sent_coef, members)
        sent = jnp.where(near, later[0] + coef * later[1], state + coef * later[0])
        came = moved(sent.astype(jnp.bfloat16), chip_swap).astype(jnp.float32)
        suffix = near_coef * later[0] + far_coef * later[1] + came
        within = odd_state + halves(link_odd, members) * suffix
        mine_suffix = jnp.where(even, within, suffix).astype(jnp.bfloat16)
        send_suffix = jnp.where(even, suffix, within).astype(jnp.bfloat16)
        other_suffix = moved(send_suffix, core_swap)
        skipped = 0
        for n in members:
            outs = finish_of(
                side_arr,
                key_rows,
                value_rows,
                *inner[n],
                mine_suffix,
                other_suffix,
                pack,
                outs,
                starts[n],
                CHUNKS[n],
                skipped,
            )
            skipped += CHUNKS[n] // 2
    return (out, *outs)


def solution(mesh):
    rows = P("pipe", "ctx", None)
    return jax.shard_map(
        on_device,
        mesh=mesh,
        in_specs=(
            rows,
            rows,
            rows,
            rows,
            P("pipe", None, "ctx"),
            P("pipe", "ctx"),
            P("pipe", "ctx", None, None, None),
        ),
        out_specs=(rows, rows, rows),
        check_vma=False,
    )
```

time: 373 us -> 159 us (0.43)
  the two profiles are of different devices: /device:TPU:0 before, /device:TPU:9 now
where the time goes in v1:
time: 159 us; the launch traced here: 158 us
  Pallas kernels  47.9 us (30%)
  waiting for transfers between devices  47.8 us (30%)
  starting transfers between devices  36.7 us (23%)
  local copies, waits for them, and re-layouts  15.3 us (10%)
  other arithmetic  6.2 us (4%)
  between operations  4.21 us (3%)
    pallas_call x9, Pallas kernels, call(): pl.pallas_call(kernel, out_shape=tuple(out_shapes), grid_spec=pltpu.Prefe...  47.9 us
    ppermute x14, waiting for transfers between devices, moved(): return lax.ppermute(value, 'ctx', pairs)  32.8 us
    ppermute x14, starting transfers between devices, moved(): return lax.ppermute(value, 'ctx', pairs)  22.4 us
    ppermute x4, waiting for transfers between devices, on_device(): grads.append(lax.ppermute(part, 'pipe', back))  15 us
    ppermute x4, starting transfers between devices, on_device(): grads.append(lax.ppermute(part, 'pipe', back))  8.36 us
    slice x4, local copies, waits for them, and re-layouts, on_device(): lax.slice_in_dim(after(next_grads, ready), start * D, (start + size) * D,...  6.92 us
    unnamed x20, local copies, waits for them, and re-layouts  6.02 us
    ppermute x1, starting transfers between devices, on_device(): lax.ppermute(docs[-1:] + 1, 'ctx', [(i, i + 1) for i in range(ctx - 1)])[0]  5.92 us
  transfers between devices with their start and end apart: 19, of which 7 were waited for; matrix products, arithmetic and copies ran while one was open for 8% of the time, Pallas kernels for 28%

profile of v1, /device:TPU:9, one launch (start us, length us, event | category | flops | bytes accessed | tf_op | source)
XLA Modules:
  0.0 158.5 jit_solution(12218427982203829268)
XLA Ops:
  0.6 1.3 fusion.29
  2.6 5.9 %collective-permute-start = (s32[1]{0:T(128)}, s32[1]{0:T(128)}, u32[]{:S(2)}, u32[]{:S(2)}) collective-permute-start(s32[1]{0:T(128)} %bitcast.1), channel_id=1, source_target_pairs={{0,1},{1,2},{2,3},{3,4},{4,5},{5,6},{6,7},{7,8},{8,9},{9,10},{10,1... | collective-permute-start | bytes 20 | tf_op jit(solution)/shard_map/ppermute | solution.py:230
  8.5 0.7 reduce.1
  9.2 0.4 convolution_bitcast_fusion
  9.6 0.2 slice_reduce_fusion
  11.7 0.9 fusion.8.mask_ref
  13.4 2.0 %fusion.18 = (f32[384]{0:T(512)S(1)}, f32[384]{0:T(512)S(1)}) fusion(pred[]{:T(512)S(6)} %eq.46, s32[1,384]{1,0:T(1,128)} %param.12, s32[]{:T(128)} %bitcast.3, s32[]{:T(128)} %bitcast.4), kind=kLoop, calls=%fused_computation.49 | loop fusion | flops 1920 | bytes 4617 | tf_op jit(solution)/shard_map/jit(_where)/select_n | solution.py:243
  15.5 0.1 collective-permute-start.3
  15.6 2.5 %slice.65 = bf16[1,384,1536]{2,1,0:T(8,128)(2,1)} slice(bf16[1,384,4096]{2,1,0:T(8,128)(2,1)} %param.10), slice={[0:1], [0:384], [0:1536]} | slice | bytes 2359296 | tf_op jit(solution)/shard_map/slice | solution.py:263
  18.1 3.8 %collective-permute-start.1 = (bf16[1,384,1536]{2,1,0:T(8,128)(2,1)}, bf16[1,384,1536]{2,1,0:T(8,128)(2,1)}, u32[]{:S(2)}, u32[]{:S(2)}) collective-permute-start(bf16[1,384,1536]{2,1,0:T(8,128)(2,1)} %slice.65), channel_id=1, source_target_pairs={{16,0},{32,16},{48,32},{64,48},{80,64},{96,80},{112,96},{0,112},{1... | collective-permute-start | bytes 3538952 | tf_op jit(solution)/shard_map/ppermute | solution.py:264
  21.9 2.4 %slice.70 = bf16[1,384,1536]{2,1,0:T(8,128)(2,1)} slice(bf16[1,384,4096]{2,1,0:T(8,128)(2,1)} %param.10), slice={[0:1], [0:384], [1536:3072]} | slice | bytes 2359296 | tf_op jit(solution)/shard_map/slice | solution.py:263
  24.2 0.1 collective-permute-start.7
  24.4 0.1 exponential_multiply_fusion.1
  24.5 0.1 maximum_maximum_fusion.pack_ref
  24.6 1.3 collective-permute-start.5
  25.9 2.1 %collective-permute-start.4 = (f32[32]{0:T(128)S(1)}, f32[32]{0:T(128)S(1)}, u32[]{:S(2)}, u32[]{:S(2)}) collective-permute-start(f32[32]{0:T(128)S(1)} %get-tuple-element.75), channel_id=1, source_target_pairs={{4,0},{5,1},{6,2},{7,3},{8,4},{9,5},{10,6},{11,7},{12,8},{13,9},{1... | collective-permute-start | bytes 392 | tf_op jit(solution)/shard_map/ppermute | solution.py:208
  28.0 0.1 dynamic-slice_bitcast_fusion.17
  28.1 0.1 maximum_bitcast_fusion.1
  28.2 0.1 dynamic-slice_bitcast_fusion.5
  28.3 0.1 maximum_bitcast_fusion.7
  28.4 2.0 %collective-permute-done.5 = f32[32]{0:T(128)S(1)} collective-permute-done((f32[32]{0:T(128)S(1)}, f32[32]{0:T(128)S(1)}, u32[]{:S(2)}, u32[]{:S(2)}) %collective-permute-start.5) | collective-permute-done | bytes 160 | tf_op jit(solution)/shard_map/ppermute | solution.py:208
  30.4 0.7 collective-permute-done.4
  31.1 1.0 slice.69
  32.2 15.0 %collective-permute-done.1.g_ref = bf16[1,384,1536]{2,1,0:T(8,128)(2,1)} collective-permute-done((bf16[1,384,1536]{2,1,0:T(8,128)(2,1)}, bf16[1,384,1536]{2,1,0:T(8,128)(2,1)}, u32[]{:S(2)}, u32[]{:S(2)}) %collective-permute-start.1) | collective-permute-done | bytes 1179680 | tf_op jit(solution)/shard_map/ppermute | solution.py:264
  47.2 1.0 slice.66
  48.2 4.4 %collective-permute-start.2 = (bf16[1,384,512]{2,1,0:T(8,128)(2,1)S(1)}, bf16[1,384,512]{2,1,0:T(8,128)(2,1)S(1)}, u32[]{:S(2)}, u32[]{:S(2)}) collective-permute-start(bf16[1,384,512]{2,1,0:T(8,128)(2,1)S(1)} %slice.66), channel_id=1, source_target_pairs={{16,0},{32,16},{48,32},{64,48},{80,64},{96,80},{112,96},{0,112},{1... | collective-permute-start | bytes 1179656 | tf_op jit(solution)/shard_map/ppermute | solution.py:264
  52.7 2.7 %collective-permute-start.9 = (f32[3,32]{1,0:T(4,128)S(1)}, f32[3,32]{1,0:T(4,128)S(1)}, u32[]{:S(2)}, u32[]{:S(2)}) collective-permute-start(f32[3,32]{1,0:T(4,128)S(1)} %pad_maximum_fusion.4), channel_id=1, source_target_pairs={{0,2},{1,3},{2,0},{3,1},{4,6},{5,7},{6,4},{7,5},{8,10},{9,11},{10,... | collective-permute-start | bytes 1160 | tf_op jit(solution)/shard_map/ppermute | solution.py:208
  55.4 1.9 %copy-done.3 = bf16[1,384,4096]{2,1,0:T(8,128)(2,1)S(1)} copy-done((bf16[1,384,4096]{2,1,0:T(8,128)(2,1)S(1)}, bf16[1,384,4096]{2,1,0:T(8,128)(2,1)}, u32[]{:S(2)}) %copy-start.3) | copy-done | bytes 3145752
  57.3 1.6 %copy-done.4 = f32[1,1,32,128,128]{4,3,2,1,0:T(8,128)S(1)} copy-done((f32[1,1,32,128,128]{4,3,2,1,0:T(8,128)S(1)}, f32[1,1,32,128,128]{4,3,2,1,0:T(8,128)}, u32[]{:S(2)}) %copy-start.4) | copy-done | bytes 2097176
  58.9 1.1 copy-done.6
  60.0 13.0 %inner_grads.4 = (bf16[1,384,4096]{2,1,0:T(8,128)(2,1)}, f32[384,1536]{1,0:T(8,128)S(1)}, f32[384,1536]{1,0:T(8,128)S(1)}, f32[12,128,128]{2,1,0:T(8,128)S(1)}) custom-call(s32[1]{0:T(128)} %bitcast.side_ref, bf16[1,384,4096]{2,1,0:T(8,128)(2,1)S(1)} %copy-done.3, bf16[1,384,4096]{2,1,0:T(8,128)(2,1)S(1)} %copy-done.1, bf16[1,384,4096]{2,1,0:T(8,128)(2,1)} %v_ref.15, ...), custom_call_target="tpu_custom_call" | custom-call | flops 1660944384 | bytes 10616832 | tf_op jit(solution)/shard_map/inner_grads/pallas_call | solution.py:73
  73.0 13.0 %inner_grads.5 = (bf16[1,384,4096]{2,1,0:T(8,128)(2,1)}, f32[384,1536]{1,0:T(8,128)S(1)}, f32[384,1536]{1,0:T(8,128)S(1)}, f32[12,128,128]{2,1,0:T(8,128)S(1)}) custom-call(s32[1]{0:T(128)} %bitcast.side_ref, bf16[1,384,4096]{2,1,0:T(8,128)(2,1)S(1)} %copy-done.3, bf16[1,384,4096]{2,1,0:T(8,128)(2,1)S(1)} %copy-done.1, ...), custom_call_target="tpu_custom_call", output_to_operand_aliasing={{0}: (8, {})} | custom-call | flops 1660944384 | bytes 10616832 | tf_op jit(solution)/shard_map/inner_grads/pallas_call | solution.py:73
  86.0 1.4 copy-done.8
  87.4 4.4 %inner_grads.6 = (bf16[1,384,4096]{2,1,0:T(8,128)(2,1)}, f32[384,512]{1,0:T(8,128)S(1)}, f32[384,512]{1,0:T(8,128)S(1)}, f32[4,128,128]{2,1,0:T(8,128)S(1)}) custom-call(s32[1]{0:T(128)} %bitcast.side_ref, bf16[1,384,4096]{2,1,0:T(8,128)(2,1)S(1)} %copy-done.3, bf16[1,384,4096]{2,1,0:T(8,128)(2,1)S(1)} %copy-done.1, ...), custom_call_target="tpu_custom_call", output_to_operand_aliasing={{0}: (8, {})} | custom-call | flops 553648128 | bytes 3538944 | tf_op jit(solution)/shard_map/inner_grads/pallas_call | solution.py:73
  91.9 1.1 head_states.1
  93.1 2.6 %collective-permute-start.8 = (f32[4,128,128]{2,1,0:T(8,128)S(1)}, f32[4,128,128]{2,1,0:T(8,128)S(1)}, u32[]{:S(2)}, u32[]{:S(2)}) collective-permute-start(f32[4,128,128]{2,1,0:T(8,128)S(1)} %pad_maximum_fusion.3), channel_id=1, source_target_pairs={{0,1},{1,0},{2,3},{3,2},{4,5},{5,4},{6,7},{7,6},{8,9},{9,8},{10,11... | collective-permute-start | bytes 786440 | tf_op jit(solution)/shard_map/ppermute | solution.py:208
  95.7 0.1 fusion.25
  95.8 0.1 collective-permute-start.14
  95.9 0.9 collective-permute-done.8
  96.8 0.1 fusion.23
  96.9 1.3 collective-permute-start.11
  98.2 2.1 %collective-permute-start.10 = (bf16[4,128,128]{2,1,0:T(8,128)(2,1)S(1)}, bf16[4,128,128]{2,1,0:T(8,128)(2,1)S(1)}, u32[]{:S(2)}, u32[]{:S(2)}) collective-permute-start(bf16[4,128,128]{2,1,0:T(8,128)(2,1)S(1)} %get-tuple-element.73), channel_id=1, source_target_pairs={{4,0},{5,1},{6,2},{7,3},{8,4},{9,5},{10,6},{11,7},{12,8},{13,9},{1... | collective-permute-start | bytes 393224 | tf_op jit(solution)/shard_map/ppermute | solution.py:208
  100.4 0.1 dynamic-slice_bitcast_fusion.7
  100.5 0.1 maximum_bitcast_fusion.6
  100.8 0.3 fusion.22
  101.0 1.3 collective-permute-start.16
  102.3 1.9 %collective-permute-start.15 = (bf16[12,128,128]{2,1,0:T(8,128)(2,1)S(1)}, bf16[12,128,128]{2,1,0:T(8,128)(2,1)S(1)}, u32[]{:S(2)}, u32[]{:S(2)}) collective-permute-start(bf16[12,128,128]{2,1,0:T(8,128)(2,1)S(1)} %get-tuple-element.71), channel_id=1, source_target_pairs={{4,0},{5,1},{6,2},{7,3},{8,4},{9,5},{10,6},{11,7},{12,8},{13,9},{1... | collective-permute-start | bytes 1179656 | tf_op jit(solution)/shard_map/ppermute | solution.py:208
  104.4 0.1 maximum_bitcast_fusion.9
  104.6 11.8 %collective-permute-done.16 = bf16[12,128,128]{2,1,0:T(8,128)(2,1)S(1)} collective-permute-done((bf16[12,128,128]{2,1,0:T(8,128)(2,1)S(1)}, bf16[12,128,128]{2,1,0:T(8,128)(2,1)S(1)}, u32[]{:S(2)}, u32[]{:S(2)}) %collective-permute-start.16) | collective-permute-done | bytes 393248 | tf_op jit(solution)/shard_map/ppermute | solution.py:208
  116.4 9.1 %collective-permute-done.15 = bf16[12,128,128]{2,1,0:T(8,128)(2,1)S(1)} collective-permute-done((bf16[12,128,128]{2,1,0:T(8,128)(2,1)S(1)}, bf16[12,128,128]{2,1,0:T(8,128)(2,1)S(1)}, u32[]{:S(2)}, u32[]{:S(2)}) %collective-permute-start.15) | collective-permute-done | bytes 393248 | tf_op jit(solution)/shard_map/ppermute | solution.py:208
  125.4 0.3 fusion.3
  125.7 1.8 %collective-permute-start.17 = (bf16[12,128,128]{2,1,0:T(8,128)(2,1)S(1)}, bf16[12,128,128]{2,1,0:T(8,128)(2,1)S(1)}, u32[]{:S(2)}, u32[]{:S(2)}) collective-permute-start(bf16[12,128,128]{2,1,0:T(8,128)(2,1)S(1)} %fusion.3), channel_id=1, source_target_pairs={{0,2},{1,3},{2,0},{3,1},{4,6},{5,7},{6,4},{7,5},{8,10},{9,11},{10,... | collective-permute-start | bytes 1179656 | tf_op jit(solution)/shard_map/ppermute | solution.py:208
  127.7 0.1 fusion.14
  127.8 1.4 collective-permute-start.12
  129.2 8.4 %collective-permute-done.17 = bf16[12,128,128]{2,1,0:T(8,128)(2,1)S(1)} collective-permute-done((bf16[12,128,128]{2,1,0:T(8,128)(2,1)S(1)}, bf16[12,128,128]{2,1,0:T(8,128)(2,1)S(1)}, u32[]{:S(2)}, u32[]{:S(2)}) %collective-permute-start.17) | collective-permute-done | bytes 393248 | tf_op jit(solution)/shard_map/ppermute | solution.py:208
  137.5 0.5 select_convert_fusion
  138.0 2.3 %collective-permute-start.18 = (bf16[12,128,128]{2,1,0:T(8,128)(2,1)S(1)}, bf16[12,128,128]{2,1,0:T(8,128)(2,1)S(1)}, u32[]{:S(2)}, u32[]{:S(2)}) collective-permute-start(bf16[12,128,128]{2,1,0:T(8,128)(2,1)S(1)} %get-tuple-element.78), channel_id=1, source_target_pairs={{0,1},{1,0},{2,3},{3,2},{4,5},{5,4},{6,7},{7,6},{8,9},{9,8},{10,11... | collective-permute-start | bytes 1179656 | tf_op jit(solution)/shard_map/ppermute | solution.py:208
  140.4 0.2 select_convert_fusion.2
  140.6 1.5 collective-permute-start.13
  142.1 3.9 %inner_grads.7 = (bf16[1,384,4096]{2,1,0:T(8,128)(2,1)}, f32[384,512]{1,0:T(8,128)S(1)}, f32[384,512]{1,0:T(8,128)S(1)}) custom-call(s32[1]{0:T(128)} %bitcast.side_ref, bf16[1,384,4096]{2,1,0:T(8,128)(2,1)S(1)} %copy-done.3, bf16[1,384,4096]{2,1,0:T(8,128)(2,1)S(1)} %copy-done.1, ...), custom_call_target="tpu_custom_call", output_to_operand_aliasing={{0}: (8, {})} | custom-call | flops 553648128 | bytes 3538944 | tf_op jit(solution)/shard_map/inner_grads/pallas_call | solution.py:73
  146.0 4.4 %finish_grads.4 = (bf16[1,384,4096]{2,1,0:T(8,128)(2,1)}, bf16[1,384,4096]{2,1,0:T(8,128)(2,1)}) custom-call(s32[1]{0:T(128)} %bitcast.side_ref, bf16[1,384,4096]{2,1,0:T(8,128)(2,1)S(1)} %copy-done.1, bf16[1,384,4096]{2,1,0:T(8,128)(2,1)S(1)} %copy-done.2, f32[384,1536]{1,0:T(8,128)S(1)} %get-tuple-element.59.ki_ref, ...), custom_call_target="tpu_custom_call" | custom-call | flops 301989888 | bytes 9437184 | tf_op jit(solution)/shard_map/finish_grads/pallas_call | solution.py:73
  150.4 4.4 %finish_grads.5 = (bf16[1,384,4096]{2,1,0:T(8,128)(2,1)}, bf16[1,384,4096]{2,1,0:T(8,128)(2,1)}) custom-call(s32[1]{0:T(128)} %bitcast.side_ref, bf16[1,384,4096]{2,1,0:T(8,128)(2,1)S(1)} %copy-done.1, bf16[1,384,4096]{2,1,0:T(8,128)(2,1)S(1)} %copy-done.2, f32[384,1536]{1,0:T(8,128)S(1)} %get-tuple-element.54.ki_ref, ...), custom_call_target="tpu_custom_call", output_to_operand_aliasing={{0}: (8, {}), {1}: (9, {})} | custom-call | flops 301989888 | bytes 9437184 | tf_op jit(solution)/shard_map/finish_grads/pallas_call | solution.py:73
  154.8 1.8 %finish_grads.6 = (bf16[1,384,4096]{2,1,0:T(8,128)(2,1)}, bf16[1,384,4096]{2,1,0:T(8,128)(2,1)}) custom-call(s32[1]{0:T(128)} %bitcast.side_ref, bf16[1,384,4096]{2,1,0:T(8,128)(2,1)S(1)} %copy-done.1, bf16[1,384,4096]{2,1,0:T(8,128)(2,1)S(1)} %copy-done.2, f32[384,512]{1,0:T(8,128)S(1)} %get-tuple-element.52.ki_ref, ...), custom_call_target="tpu_custom_call", output_to_operand_aliasing={{0}: (8, {}), {1}: (9, {})} | custom-call | flops 100663296 | bytes 3145728 | tf_op jit(solution)/shard_map/finish_grads/pallas_call | solution.py:73
  156.6 1.8 %finish_grads.7 = (bf16[1,384,4096]{2,1,0:T(8,128)(2,1)}, bf16[1,384,4096]{2,1,0:T(8,128)(2,1)}) custom-call(s32[1]{0:T(128)} %bitcast.side_ref, bf16[1,384,4096]{2,1,0:T(8,128)(2,1)S(1)} %copy-done.1, bf16[1,384,4096]{2,1,0:T(8,128)(2,1)S(1)} %copy-done.2, f32[384,512]{1,0:T(8,128)S(1)} %get-tuple-element.49.ki_ref, ...), custom_call_target="tpu_custom_call", output_to_operand_aliasing={{0}: (8, {}), {1}: (9, {})} | custom-call | flops 100663296 | bytes 3145728 | tf_op jit(solution)/shard_map/finish_grads/pallas_call | solution.py:73
  (53 shorter events, 1.3 us)
Async XLA Ops:
  0.6 8.6 %copy-start = (f32[1,32,384]{2,1,0:T(8,128)S(1)}, f32[1,32,384]{2,1,0:T(8,128)}, u32[]{:S(2)}) copy-start(f32[1,32,384]{2,1,0:T(8,128)} %param.11) | copy-start | bytes 147460
  2.6 10.2 %collective-permute-start = (s32[1]{0:T(128)}, s32[1]{0:T(128)}, u32[]{:S(2)}, u32[]{:S(2)}) collective-permute-start(s32[1]{0:T(128)} %bitcast.1), channel_id=1, source_target_pairs={{0,1},{1,2},{2,3},{3,4},{4,5},{5,6},{6,7},{7,8},{8,9},{9,10},{10,1... | collective-permute-start | bytes 20 | tf_op jit(solution)/shard_map/ppermute | solution.py:230
  15.5 40.0 %copy-start.1 = (bf16[1,384,4096]{2,1,0:T(8,128)(2,1)S(1)}, bf16[1,384,4096]{2,1,0:T(8,128)(2,1)}, u32[]{:S(2)}) copy-start(bf16[1,384,4096]{2,1,0:T(8,128)(2,1)} %k_ref.15) | copy-start | bytes 9437188
  15.5 6.4 %collective-permute-start.3 = (f32[32]{0:T(128)S(1)}, f32[32]{0:T(128)S(1)}, u32[]{:S(2)}, u32[]{:S(2)}) collective-permute-start(f32[32]{0:T(128)S(1)} %broadcast_select_fusion.5), channel_id=1, source_target_pairs={{0,1},{1,0},{2,3},{3,2},{4,5},{5,4},{6,7},{7,6},{8,9},{9,8},{10,11... | collective-permute-start | bytes 392 | tf_op jit(solution)/shard_map/ppermute | solution.py:208
  18.1 29.1 %collective-permute-start.1 = (bf16[1,384,1536]{2,1,0:T(8,128)(2,1)}, bf16[1,384,1536]{2,1,0:T(8,128)(2,1)}, u32[]{:S(2)}, u32[]{:S(2)}) collective-permute-start(bf16[1,384,1536]{2,1,0:T(8,128)(2,1)} %slice.65), channel_id=1, source_target_pairs={{16,0},{32,16},{48,32},{64,48},{80,64},{96,80},{112,96},{0,112},{1... | collective-permute-start | bytes 3538952 | tf_op jit(solution)/shard_map/ppermute | solution.py:264
  24.2 48.7 %collective-permute-start.7 = (bf16[1,384,1536]{2,1,0:T(8,128)(2,1)}, bf16[1,384,1536]{2,1,0:T(8,128)(2,1)}, u32[]{:S(2)}, u32[]{:S(2)}) collective-permute-start(bf16[1,384,1536]{2,1,0:T(8,128)(2,1)} %slice.70), channel_id=1, source_target_pairs={{16,0},{32,16},{48,32},{64,48},{80,64},{96,80},{112,96},{0,112},{1... | collective-permute-start | bytes 3538952 | tf_op jit(solution)/shard_map/ppermute | solution.py:264
  24.6 5.8 %collective-permute-start.5 = (f32[32]{0:T(128)S(1)}, f32[32]{0:T(128)S(1)}, u32[]{:S(2)}, u32[]{:S(2)}) collective-permute-start(f32[32]{0:T(128)S(1)} %get-tuple-element.75), channel_id=1, source_target_pairs={{8,0},{9,1},{10,2},{11,3},{12,4},{13,5},{14,6},{15,7},{24,16},{25,... | collective-permute-start | bytes 392 | tf_op jit(solution)/shard_map/ppermute | solution.py:208
  25.9 5.2 %collective-permute-start.4 = (f32[32]{0:T(128)S(1)}, f32[32]{0:T(128)S(1)}, u32[]{:S(2)}, u32[]{:S(2)}) collective-permute-start(f32[32]{0:T(128)S(1)} %get-tuple-element.75), channel_id=1, source_target_pairs={{4,0},{5,1},{6,2},{7,3},{8,4},{9,5},{10,6},{11,7},{12,8},{13,9},{1... | collective-permute-start | bytes 392 | tf_op jit(solution)/shard_map/ppermute | solution.py:208
  32.2 55.3 %collective-permute-start.6 = (bf16[1,384,512]{2,1,0:T(8,128)(2,1)S(1)}, bf16[1,384,512]{2,1,0:T(8,128)(2,1)S(1)}, u32[]{:S(2)}, u32[]{:S(2)}) collective-permute-start(bf16[1,384,512]{2,1,0:T(8,128)(2,1)S(1)} %slice.69), channel_id=1, source_target_pairs={{16,0},{32,16},{48,32},{64,48},{80,64},{96,80},{112,96},{0,112},{1... | collective-permute-start | bytes 1179656 | tf_op jit(solution)/shard_map/ppermute | solution.py:264
  48.2 43.7 %collective-permute-start.2 = (bf16[1,384,512]{2,1,0:T(8,128)(2,1)S(1)}, bf16[1,384,512]{2,1,0:T(8,128)(2,1)S(1)}, u32[]{:S(2)}, u32[]{:S(2)}) collective-permute-start(bf16[1,384,512]{2,1,0:T(8,128)(2,1)S(1)} %slice.66), channel_id=1, source_target_pairs={{16,0},{32,16},{48,32},{64,48},{80,64},{96,80},{112,96},{0,112},{1... | collective-permute-start | bytes 1179656 | tf_op jit(solution)/shard_map/ppermute | solution.py:264
  52.7 47.7 %collective-permute-start.9 = (f32[3,32]{1,0:T(4,128)S(1)}, f32[3,32]{1,0:T(4,128)S(1)}, u32[]{:S(2)}, u32[]{:S(2)}) collective-permute-start(f32[3,32]{1,0:T(4,128)S(1)} %pad_maximum_fusion.4), channel_id=1, source_target_pairs={{0,2},{1,3},{2,0},{3,1},{4,6},{5,7},{6,4},{7,5},{8,10},{9,11},{10,... | collective-permute-start | bytes 1160 | tf_op jit(solution)/shard_map/ppermute | solution.py:208
  55.4 1.9 %copy-start.3 = (bf16[1,384,4096]{2,1,0:T(8,128)(2,1)S(1)}, bf16[1,384,4096]{2,1,0:T(8,128)(2,1)}, u32[]{:S(2)}) copy-start(bf16[1,384,4096]{2,1,0:T(8,128)(2,1)} %q_ref.9) | copy-start | bytes 9437188
  57.3 1.6 %copy-start.4 = (f32[1,1,32,128,128]{4,3,2,1,0:T(8,128)S(1)}, f32[1,1,32,128,128]{4,3,2,1,0:T(8,128)}, u32[]{:S(2)}) copy-start(f32[1,1,32,128,128]{4,3,2,1,0:T(8,128)} %p_ref.7) | copy-start | bytes 6291460
  58.9 1.1 copy-start.6
  60.0 13.0 %copy-start.5 = (f32[1,1,32,128,128]{4,3,2,1,0:T(8,128)S(1)}, f32[1,1,32,128,128]{4,3,2,1,0:T(8,128)}, u32[]{:S(2)}) copy-start(f32[1,1,32,128,128]{4,3,2,1,0:T(8,128)} %p_ref.7) | copy-start | bytes 6291460
  60.0 13.0 %copy-start.7 = (f32[384,384]{1,0:T(8,128)S(1)}, f32[384,384]{1,0:T(8,128)}, u32[]{:S(2)}) copy-start(f32[384,384]{1,0:T(8,128)} %fusion.8.mask_ref) | copy-start | bytes 1769476
  73.0 14.5 %copy-start.2 = (bf16[1,384,4096]{2,1,0:T(8,128)(2,1)S(1)}, bf16[1,384,4096]{2,1,0:T(8,128)(2,1)}, u32[]{:S(2)}) copy-start(bf16[1,384,4096]{2,1,0:T(8,128)(2,1)} %v_ref.15) | copy-start | bytes 9437188
  86.0 1.4 copy-start.8
  93.1 3.7 %collective-permute-start.8 = (f32[4,128,128]{2,1,0:T(8,128)S(1)}, f32[4,128,128]{2,1,0:T(8,128)S(1)}, u32[]{:S(2)}, u32[]{:S(2)}) collective-permute-start(f32[4,128,128]{2,1,0:T(8,128)S(1)} %pad_maximum_fusion.3), channel_id=1, source_target_pairs={{0,1},{1,0},{2,3},{3,2},{4,5},{5,4},{6,7},{7,6},{8,9},{9,8},{10,11... | collective-permute-start | bytes 786440 | tf_op jit(solution)/shard_map/ppermute | solution.py:208
  95.8 4.9 %collective-permute-start.14 = (f32[12,128,128]{2,1,0:T(8,128)S(1)}, f32[12,128,128]{2,1,0:T(8,128)S(1)}, u32[]{:S(2)}, u32[]{:S(2)}) collective-permute-start(f32[12,128,128]{2,1,0:T(8,128)S(1)} %pad_maximum_fusion), channel_id=1, source_target_pairs={{0,1},{1,0},{2,3},{3,2},{4,5},{5,4},{6,7},{7,6},{8,9},{9,8},{10,11... | collective-permute-start | bytes 2359304 | tf_op jit(solution)/shard_map/ppermute | solution.py:208
  96.9 30.7 %collective-permute-start.11 = (bf16[4,128,128]{2,1,0:T(8,128)(2,1)S(1)}, bf16[4,128,128]{2,1,0:T(8,128)(2,1)S(1)}, u32[]{:S(2)}, u32[]{:S(2)}) collective-permute-start(bf16[4,128,128]{2,1,0:T(8,128)(2,1)S(1)} %get-tuple-element.73), channel_id=1, source_target_pairs={{8,0},{9,1},{10,2},{11,3},{12,4},{13,5},{14,6},{15,7},{24,16},{25,... | collective-permute-start | bytes 393224 | tf_op jit(solution)/shard_map/ppermute | solution.py:208
  98.2 29.4 %collective-permute-start.10 = (bf16[4,128,128]{2,1,0:T(8,128)(2,1)S(1)}, bf16[4,128,128]{2,1,0:T(8,128)(2,1)S(1)}, u32[]{:S(2)}, u32[]{:S(2)}) collective-permute-start(bf16[4,128,128]{2,1,0:T(8,128)(2,1)S(1)} %get-tuple-element.73), channel_id=1, source_target_pairs={{4,0},{5,1},{6,2},{7,3},{8,4},{9,5},{10,6},{11,7},{12,8},{13,9},{1... | collective-permute-start | bytes 393224 | tf_op jit(solution)/shard_map/ppermute | solution.py:208
  101.0 15.3 %collective-permute-start.16 = (bf16[12,128,128]{2,1,0:T(8,128)(2,1)S(1)}, bf16[12,128,128]{2,1,0:T(8,128)(2,1)S(1)}, u32[]{:S(2)}, u32[]{:S(2)}) collective-permute-start(bf16[12,128,128]{2,1,0:T(8,128)(2,1)S(1)} %get-tuple-element.71), channel_id=1, source_target_pairs={{8,0},{9,1},{10,2},{11,3},{12,4},{13,5},{14,6},{15,7},{24,16},{25,... | collective-permute-start | bytes 1179656 | tf_op jit(solution)/shard_map/ppermute | solution.py:208
  102.3 23.1 %collective-permute-start.15 = (bf16[12,128,128]{2,1,0:T(8,128)(2,1)S(1)}, bf16[12,128,128]{2,1,0:T(8,128)(2,1)S(1)}, u32[]{:S(2)}, u32[]{:S(2)}) collective-permute-start(bf16[12,128,128]{2,1,0:T(8,128)(2,1)S(1)} %get-tuple-element.71), channel_id=1, source_target_pairs={{4,0},{5,1},{6,2},{7,3},{8,4},{9,5},{10,6},{11,7},{12,8},{13,9},{1... | collective-permute-start | bytes 1179656 | tf_op jit(solution)/shard_map/ppermute | solution.py:208
  125.7 11.8 %collective-permute-start.17 = (bf16[12,128,128]{2,1,0:T(8,128)(2,1)S(1)}, bf16[12,128,128]{2,1,0:T(8,128)(2,1)S(1)}, u32[]{:S(2)}, u32[]{:S(2)}) collective-permute-start(bf16[12,128,128]{2,1,0:T(8,128)(2,1)S(1)} %fusion.3), channel_id=1, source_target_pairs={{0,2},{1,3},{2,0},{3,1},{4,6},{5,7},{6,4},{7,5},{8,10},{9,11},{10,... | collective-permute-start | bytes 1179656 | tf_op jit(solution)/shard_map/ppermute | solution.py:208
  127.8 12.6 %collective-permute-start.12 = (bf16[4,128,128]{2,1,0:T(8,128)(2,1)S(1)}, bf16[4,128,128]{2,1,0:T(8,128)(2,1)S(1)}, u32[]{:S(2)}, u32[]{:S(2)}) collective-permute-start(bf16[4,128,128]{2,1,0:T(8,128)(2,1)S(1)} %fusion.14), channel_id=1, source_target_pairs={{0,2},{1,3},{2,0},{3,1},{4,6},{5,7},{6,4},{7,5},{8,10},{9,11},{10,... | collective-permute-start | bytes 393224 | tf_op jit(solution)/shard_map/ppermute | solution.py:208
  138.0 8.0 %collective-permute-start.18 = (bf16[12,128,128]{2,1,0:T(8,128)(2,1)S(1)}, bf16[12,128,128]{2,1,0:T(8,128)(2,1)S(1)}, u32[]{:S(2)}, u32[]{:S(2)}) collective-permute-start(bf16[12,128,128]{2,1,0:T(8,128)(2,1)S(1)} %get-tuple-element.78), channel_id=1, source_target_pairs={{0,1},{1,0},{2,3},{3,2},{4,5},{5,4},{6,7},{7,6},{8,9},{9,8},{10,11... | collective-permute-start | bytes 1179656 | tf_op jit(solution)/shard_map/ppermute | solution.py:208
  140.6 14.2 %collective-permute-start.13 = (bf16[4,128,128]{2,1,0:T(8,128)(2,1)S(1)}, bf16[4,128,128]{2,1,0:T(8,128)(2,1)S(1)}, u32[]{:S(2)}, u32[]{:S(2)}) collective-permute-start(bf16[4,128,128]{2,1,0:T(8,128)(2,1)S(1)} %get-tuple-element.80), channel_id=1, source_target_pairs={{0,1},{1,0},{2,3},{3,2},{4,5},{5,4},{6,7},{7,6},{8,9},{9,8},{10,11... | collective-permute-start | bytes 393224 | tf_op jit(solution)/shard_map/ppermute | solution.py:208
  146.0 4.4 %copy-start.9 = (f32[384,1536]{1,0:T(8,128)S(1)}, f32[384,1536]{1,0:T(8,128)}, u32[]{:S(2)}) copy-start(f32[384,1536]{1,0:T(8,128)} %copy-done.8) | copy-start | bytes 7077892

commit v2 on v1

--- a/solution.py
+++ b/solution.py
@@ -8,7 +8,7 @@
 from jax.sharding import PartitionSpec as P
 
 D = 128
-GROUPS = ((12, 12), (4, 4))
+GROUPS = ((8, 12), (8, 4))
 CHUNKS = sum(GROUPS, ())
 PAIR = 2
 PACK = 8
@@ -61,7 +61,7 @@
         self.whole = pl.BlockSpec((length, length), lambda t, s: (0, 0))
 
 
-def call(kernel, name, place, side, args, specs, out_shapes, out_specs, kept, cost):
+def call(kernel, name, place, side, args, specs, out_shapes, out_specs, kept, cost, limit=VMEM_BYTES):
     args = [side, *args]
     specs = list(specs)
     aliases = {}
@@ -77,7 +77,7 @@
             num_scalar_prefetch=1, grid=(place.steps,), in_specs=specs, out_specs=list(out_specs)
         ),
         input_output_aliases=aliases,
-        compiler_params=pltpu.CompilerParams(vmem_limit_bytes=VMEM_BYTES),
+        compiler_params=pltpu.CompilerParams(vmem_limit_bytes=limit),
         cost_estimate=pl.CostEstimate(**cost),
         name=name,
     )(*args)
@@ -88,7 +88,7 @@
     at = Place(start, heads, length, True)
     state = jax.ShapeDtypeStruct((heads, D, D), jnp.float32)
     cost = dict(
-        flops=heads * length * D * D * 2, bytes_accessed=heads * length * D * 4, transcendentals=0
+        flops=heads * length * D * D * 2, bytes_accessed=heads * length * D * 26, transcendentals=0
     )
     return call(
         state_kernel,
@@ -152,7 +152,7 @@
     whole = jax.ShapeDtypeStruct(q.shape, jnp.bfloat16)
     cost = dict(
         flops=heads * 33 * 2 * D * D * D,
-        bytes_accessed=heads * length * D * 18,
+        bytes_accessed=heads * length * D * 80,
         transcendentals=heads * length * length // 2,
     )
     return call(
@@ -166,6 +166,7 @@
         (at.wide, at.flat, at.flat) + ((at.state,) if with_states else ()),
         (out,),
         cost,
+        VMEM_BYTES if start else 58 << 20,
     )
 
 
@@ -188,7 +189,7 @@
     at = Place(start, heads, length, False, skipped)
     whole = jax.ShapeDtypeStruct(k.shape, jnp.bfloat16)
     cost = dict(
-        flops=heads * 6 * 2 * D * D * D, bytes_accessed=heads * length * D * 16, transcendentals=0
+        flops=heads * 6 * 2 * D * D * D, bytes_accessed=heads * length * D * 30, transcendentals=0
     )
     return call(
         finish_kernel,
@@ -227,7 +228,11 @@
 
     starts = [sum(CHUNKS[:n]) for n in range(len(CHUNKS))]
     docs = doc_ids[0]
+    opening = lax.slice_in_dim(next_grads, 0, CHUNKS[0] * D, axis=2)
+    grads = [lax.ppermute(opening, "pipe", back)]
+    docs, log_decay = lax.optimization_barrier((docs, log_decay, opening))[:2]
     prior = lax.ppermute(docs[-1:] + 1, "ctx", [(i, i + 1) for i in range(ctx - 1)])[0]
+
     place = lax.axis_index("ctx")
     side = place % 2
     pair = (place // 2) % 2
@@ -250,18 +255,11 @@
         axis=1,
     )
     link = jnp.where((docs[0] == docs[-1]) & continues, jnp.exp(running[:, -1]), 0.0)
-    partner = moved(link, core_swap)
-    link_even = jnp.where(even, link, partner)
-    link_odd = jnp.where(even, partner, link)
-    chip_link = link_even * link_odd
-    near_table = jnp.stack([chip_link] + [moved(chip_link, pairs) for pairs in row_up])
     side_arr = side.astype(jnp.int32).reshape(1)
 
-    grads = []
-    for n, (start, size) in enumerate(zip(starts, CHUNKS)):
-        ready = (prior, chip_link, near_table, grads[0] if n else None)[min(n, 3)]
-        part = lax.slice_in_dim(after(next_grads, ready), start * D, (start + size) * D, axis=2)
-        grads.append(lax.ppermute(part, "pipe", back))
+    for start, size in list(zip(starts, CHUNKS))[1:]:
+        part = lax.slice_in_dim(after(next_grads, running), start * D, (start + size) * D, axis=2)
+        grads.append(lax.ppermute(after(part, grads[0]), "pipe", back))
 
     def halves(table, members):
         return jnp.concatenate([part_of(table, starts[n] + side * (CHUNKS[n] // 2), CHUNKS[n] // 2) for n in members])
@@ -279,16 +277,30 @@
             start, size, grad = starts[n], CHUNKS[n], grads[n]
             if out is not None:
                 grad = after(grad, out)
+            if begin and n < len(CHUNKS) - 1:
+                grad = after(grad, low)
             inputs = (prefix_states, mask, pack, out, start, size)
             if n == len(CHUNKS) - 1:
                 state = states_of(side_arr, queries, grad, pack, start, size)
                 late = (n, grad, inputs)
+                before_last = out
             else:
                 out, *inner[n], state = inner_of(side_arr, queries, key_rows, value_rows, grad, *inputs, True)
             states.append(state)
+            if n == 0:
+                first_out = out
+        if begin == 0:
+            link = after(link, first_out)
+            partner = moved(link, core_swap)
+            link_even = jnp.where(even, link, partner)
+            link_odd = jnp.where(even, partner, link)
+            chip_link = link_even * link_odd
+            near_table = jnp.stack([chip_link] + [moved(chip_link, pairs) for pairs in row_up])
         other = jnp.concatenate([state[: state.shape[0] // 2] for state in states])
         mine = jnp.concatenate([state[state.shape[0] // 2 :] for state in states])
         came = moved(other, core_swap)
+        if begin:
+            came = after(came, *held[-1][3])
         even_state = jnp.where(even, mine, came)
         odd_state = jnp.where(even, came, mine)
         state = even_state + halves(link_even, members) * odd_state
@@ -299,7 +311,7 @@
             out, *inner[n] = inner_of(side_arr, queries, key_rows, value_rows, after(grad, low), *inputs, False)
         held.append((members, odd_state, state, later, inner))
 
-    beside = after(moved(near_table, chip_swap), held[-1][2])
+    beside = after(moved(near_table, chip_swap), before_last)
     near_rows = jnp.where(near, near_table, beside)
     far_rows = jnp.where(near, beside, near_table)
     far_link, next_near, next_far, last_near = far_rows[0], near_rows[1], far_rows[1], near_rows[2]
@@ -310,13 +322,14 @@
     sent_coef = jnp.where(near, next_near * next_far, far_link * next_near)
     outs = (None, None)
     for members, odd_state, state, later, inner in held:
-        if members[-1] < len(CHUNKS) - 1:
-            state = after(state, grads[-1])
+        state = after(state, out if members[-1] == len(CHUNKS) - 1 else grads[-1])
         later = [value.astype(jnp.float32) for value in later]
         near_coef, far_coef = (halves(table, members) for table in own_coef)
         coef = halves(sent_coef, members)
         sent = jnp.where(near, later[0] + coef * later[1], state + coef * later[0])
-        came = moved(sent.astype(jnp.bfloat16), chip_swap).astype(jnp.float32)
+        came = moved(sent.astype(jnp.bfloat16), chip_swap)
+        came = after(came, out) if outs[0] is None else after(came, *first_outs)
+        came = came.astype(jnp.float32)
         suffix = near_coef * later[0] + far_coef * later[1] + came
         within = odd_state + halves(link_odd, members) * suffix
         mine_suffix = jnp.where(even, within, suffix).astype(jnp.bfloat16)
@@ -338,6 +351,8 @@
                 skipped,
             )
             skipped += CHUNKS[n] // 2
+            if n == 0:
+                first_outs = outs
     return (out, *outs)
 
 

time: 159 us -> 138 us (0.87)
  waiting for transfers between devices: 47.8 us -> 23 us
  Pallas kernels: 47.9 us -> 51 us
  starting transfers between devices: 36.7 us -> 38.3 us
    ppermute x14, waiting for transfers between devices: 32.8 us -> 7 us  [moved(): return lax.ppermute(value, 'ctx', pairs)]
    ppermute x1, starting transfers between devices: 5.92 us -> 14.6 us  [on_device(): lax.ppermute(docs[-1:] + 1, 'ctx', [(i, i + 1) for i in range(ctx - 1)])[0]]
    ppermute x14, starting transfers between devices: 22.4 us -> 18.8 us  [moved(): return lax.ppermute(value, 'ctx', pairs)]
    ppermute x4, starting transfers between devices: 8.36 us -> 4.84 us  [the longest x1 4.68 us: on_device(): grads = [lax.ppermute(opening, 'pipe', back)]]
    pallas_call x9, Pallas kernels: 47.9 us -> 51 us  [call(): pl.pallas_call(kernel, out_shape=tuple(out_shapes), grid_spec=pltpu.Prefe...]
    unnamed x20 -> x30, local copies, waits for them, and re-layouts: 6.02 us -> 5.31 us
  transfers between devices with their start and end apart: 19 -> 19, of which waited for: 7 -> 6; matrix products, arithmetic and copies ran while one was open for 8% -> 10% of each run, Pallas kernels for 28% -> 33%
where the time goes in v2:
time: 138 us
  Pallas kernels  51 us (37%)
  starting transfers between devices  38.3 us (28%)
  waiting for transfers between devices  23 us (17%)
  local copies, waits for them, and re-layouts  14.6 us (11%)
  other arithmetic  6.09 us (4%)
  between operations  4.25 us (3%)
    pallas_call x9, Pallas kernels, call(): pl.pallas_call(kernel, out_shape=tuple(out_shapes), grid_spec=pltpu.Prefe...  51 us
    ppermute x14, starting transfers between devices, moved(): return lax.ppermute(value, 'ctx', pairs)  18.8 us
    ppermute x3, waiting for transfers between devices, on_device(): grads.append(lax.ppermute(after(part, grads[0]), 'pipe', back))  16 us
    ppermute x1, starting transfers between devices, on_device(): lax.ppermute(docs[-1:] + 1, 'ctx', [(i, i + 1) for i in range(ctx - 1)])[0]  14.6 us
    ppermute x14, waiting for transfers between devices, moved(): return lax.ppermute(value, 'ctx', pairs)  7 us
    unnamed x30, local copies, waits for them, and re-layouts  5.31 us
    ppermute x1, starting transfers between devices, on_device(): grads = [lax.ppermute(opening, 'pipe', back)]  4.68 us
    slice x3, local copies, waits for them, and re-layouts, on_device(): lax.slice_in_dim(after(next_grads, running), start * D, (start + size) *...  3.89 us
  transfers between devices with their start and end apart: 19, of which 6 were waited for; matrix products, arithmetic and copies ran while one was open for 10% of the time, Pallas kernels for 33%

profile of v2, /device:TPU:9, one launch (start us, length us, event | category | flops | bytes accessed | tf_op | source)
XLA Modules:
  0.0 137.6 jit_solution(16178927883076010882)
XLA Ops:
  0.7 2.2 %slice.62 = bf16[1,384,1024]{2,1,0:T(8,128)(2,1)} slice(bf16[1,384,4096]{2,1,0:T(8,128)(2,1)} %param.10), slice={[0:1], [0:384], [0:1024]} | slice | bytes 1572864 | tf_op jit(solution)/shard_map/slice | solution.py:231
  2.9 4.7 %collective-permute-start = (bf16[1,384,1024]{2,1,0:T(8,128)(2,1)}, bf16[1,384,1024]{2,1,0:T(8,128)(2,1)}, u32[]{:S(2)}, u32[]{:S(2)}) collective-permute-start(bf16[1,384,1024]{2,1,0:T(8,128)(2,1)} %slice.62), channel_id=1, source_target_pairs={{16,0},{32,16},{48,32},{64,48},{80,64},{96,80},{112,96},{0,112},{1... | collective-permute-start | bytes 2359304 | tf_op jit(solution)/shard_map/ppermute | solution.py:232
  7.6 0.7 reduce
  8.3 0.6 fusion.28
  9.5 14.6 %collective-permute-start.4 = (s32[1]{0:T(128)}, s32[1]{0:T(128)}, u32[]{:S(2)}, u32[]{:S(2)}) collective-permute-start(s32[1]{0:T(128)} %add.106), channel_id=1, source_target_pairs={{0,1},{1,2},{2,3},{3,4},{4,5},{5,6},{6,7},{7,8},{8,9},{9,10},{10,1... | collective-permute-start | bytes 20 | tf_op jit(solution)/shard_map/ppermute | solution.py:234
  24.1 0.3 fusion.5
  24.5 0.9 fusion.8.mask_ref
  25.4 1.8 %slice.63 = bf16[1,384,512]{2,1,0:T(8,128)(2,1)} slice(bf16[1,384,4096]{2,1,0:T(8,128)(2,1)} %param.10), slice={[0:1], [0:384], [3584:4096]} | slice | bytes 786432 | tf_op jit(solution)/shard_map/slice | solution.py:261
  27.2 0.9 slice.64
  28.1 1.2 slice.65
  31.3 0.2 slice_reduce_fusion
  32.2 1.3 and_select_fusion
  33.5 0.1 exponential_multiply_fusion.1
  33.6 0.8 maximum_maximum_fusion.pack_ref
  34.4 0.1 collective-permute-start.1
  34.5 0.1 collective-permute-start.2
  34.6 9.9 %inner_grads.4 = (bf16[1,384,4096]{2,1,0:T(8,128)(2,1)}, f32[384,1024]{1,0:T(8,128)}, f32[384,1024]{1,0:T(8,128)}, f32[8,128,128]{2,1,0:T(8,128)}) custom-call(s32[1]{0:T(128)} %bitcast.side_ref, bf16[1,384,4096]{2,1,0:T(8,128)(2,1)} %q_ref.9, bf16[1,384,4096]{2,1,0:T(8,128)(2,1)} %k_ref.15, bf16[1,384,4096]{2,1,0:T(8,128)(2,1)} %v_ref.15, ...), custom_call_target="tpu_custom_call" | custom-call | flops 1107296256 | bytes 31457280 | tf_op jit(solution)/shard_map/inner_grads/pallas_call | solution.py:73
  44.5 0.1 collective-permute-start.6
  44.6 1.1 fusion.26
  45.7 1.3 collective-permute-start.11
  47.0 2.1 %collective-permute-start.10 = (f32[32]{0:T(128)S(1)}, f32[32]{0:T(128)S(1)}, u32[]{:S(2)}, u32[]{:S(2)}) collective-permute-start(f32[32]{0:T(128)S(1)} %get-tuple-element.85), channel_id=1, source_target_pairs={{4,0},{5,1},{6,2},{7,3},{8,4},{9,5},{10,6},{11,7},{12,8},{13,9},{1... | collective-permute-start | bytes 392 | tf_op jit(solution)/shard_map/ppermute | solution.py:209
  49.1 0.1 dynamic-slice_bitcast_fusion.6
  49.3 0.1 dynamic-slice_bitcast_fusion.15
  49.4 13.4 %collective-permute-done.3.g_ref = bf16[1,384,1536]{2,1,0:T(8,128)(2,1)} collective-permute-done((bf16[1,384,1536]{2,1,0:T(8,128)(2,1)}, bf16[1,384,1536]{2,1,0:T(8,128)(2,1)}, u32[]{:S(2)}, u32[]{:S(2)}) %collective-permute-start.3) | collective-permute-done | bytes 1179680 | tf_op jit(solution)/shard_map/ppermute | solution.py:262
  62.8 1.9 %copy-done.3 = bf16[1,384,4096]{2,1,0:T(8,128)(2,1)S(1)} copy-done((bf16[1,384,4096]{2,1,0:T(8,128)(2,1)S(1)}, bf16[1,384,4096]{2,1,0:T(8,128)(2,1)}, u32[]{:S(2)}) %copy-start.3) | copy-done | bytes 3145752
  64.7 1.1 copy-done.6
  65.7 12.8 %inner_grads.5 = (bf16[1,384,4096]{2,1,0:T(8,128)(2,1)}, f32[384,1536]{1,0:T(8,128)S(1)}, f32[384,1536]{1,0:T(8,128)S(1)}, f32[12,128,128]{2,1,0:T(8,128)S(1)}) custom-call(s32[1]{0:T(128)} %bitcast.side_ref, bf16[1,384,4096]{2,1,0:T(8,128)(2,1)S(1)} %copy-done.3, bf16[1,384,4096]{2,1,0:T(8,128)(2,1)S(1)} %copy-done.1, ...), custom_call_target="tpu_custom_call", output_to_operand_aliasing={{0}: (8, {})} | custom-call | flops 1660944384 | bytes 47185920 | tf_op jit(solution)/shard_map/inner_grads/pallas_call | solution.py:73
  78.7 0.1 collective-permute-start.5
  78.8 0.1 dynamic-slice_bitcast_fusion.16
  78.8 0.1 maximum_bitcast_fusion.1
  79.2 2.5 %collective-permute-start.12 = (f32[3,32]{1,0:T(4,128)S(1)}, f32[3,32]{1,0:T(4,128)S(1)}, u32[]{:S(2)}, u32[]{:S(2)}) collective-permute-start(f32[3,32]{1,0:T(4,128)S(1)} %pad_maximum_fusion.4), channel_id=1, source_target_pairs={{0,2},{1,3},{2,0},{3,1},{4,6},{5,7},{6,4},{7,5},{8,10},{9,11},{10,... | collective-permute-start | bytes 1160 | tf_op jit(solution)/shard_map/ppermute | solution.py:209
  81.7 2.6 %collective-permute-done.2.g_ref = bf16[1,384,1024]{2,1,0:T(8,128)(2,1)} collective-permute-done((bf16[1,384,1024]{2,1,0:T(8,128)(2,1)}, bf16[1,384,1024]{2,1,0:T(8,128)(2,1)}, u32[]{:S(2)}, u32[]{:S(2)}) %collective-permute-start.2) | collective-permute-done | bytes 786464 | tf_op jit(solution)/shard_map/ppermute | solution.py:262
  84.3 0.2 fusion.23
  84.6 1.3 collective-permute-start.9
  85.9 1.9 %collective-permute-start.8 = (bf16[10,128,128]{2,1,0:T(8,128)(2,1)S(1)}, bf16[10,128,128]{2,1,0:T(8,128)(2,1)S(1)}, u32[]{:S(2)}, u32[]{:S(2)}) collective-permute-start(bf16[10,128,128]{2,1,0:T(8,128)(2,1)S(1)} %get-tuple-element.90), channel_id=1, source_target_pairs={{4,0},{5,1},{6,2},{7,3},{8,4},{9,5},{10,6},{11,7},{12,8},{13,9},{1... | collective-permute-start | bytes 983048 | tf_op jit(solution)/shard_map/ppermute | solution.py:209
  87.8 9.1 %inner_grads.6 = (bf16[1,384,4096]{2,1,0:T(8,128)(2,1)}, f32[384,1024]{1,0:T(8,128)S(1)}, f32[384,1024]{1,0:T(8,128)S(1)}, f32[8,128,128]{2,1,0:T(8,128)S(1)}) custom-call(s32[1]{0:T(128)} %bitcast.side_ref, bf16[1,384,4096]{2,1,0:T(8,128)(2,1)S(1)} %copy-done.3, bf16[1,384,4096]{2,1,0:T(8,128)(2,1)S(1)} %copy-done.1, ...), custom_call_target="tpu_custom_call", output_to_operand_aliasing={{0}: (8, {})} | custom-call | flops 1107296256 | bytes 31457280 | tf_op jit(solution)/shard_map/inner_grads/pallas_call | solution.py:73
  96.9 1.2 copy-done.10
  98.0 1.1 copy-done.12
  99.2 0.1 dynamic-slice_bitcast_fusion.4
  99.6 0.1 dynamic-slice_bitcast_fusion.1
  99.7 0.1 dynamic-slice_bitcast_fusion.11
  99.9 2.0 %head_states.1 = f32[4,128,128]{2,1,0:T(8,128)S(1)} custom-call(s32[1]{0:T(128)} %bitcast.side_ref, bf16[1,384,4096]{2,1,0:T(8,128)(2,1)S(1)} %copy-done.3, bf16[1,384,512]{2,1,0:T(8,128)(2,1)} %collective-permute-done.1.g_ref, f32[16,8,384]{2,1,0:T(8,128)S(1)} %copy-done.5), custom_call_target="tpu_custom_call" | custom-call | flops 50331648 | bytes 5111808 | tf_op jit(solution)/shard_map/head_states/pallas_call | solution.py:73
  101.9 0.1 collective-permute-start.7
  102.3 0.1 maximum_bitcast_fusion.7
  102.3 0.9 collective-permute-done.8
  103.2 0.3 fusion.3
  103.5 1.0 collective-permute-start.16
  104.6 0.1 fusion.22
  104.7 1.3 collective-permute-start.14
  106.0 2.1 %collective-permute-start.13 = (bf16[6,128,128]{2,1,0:T(8,128)(2,1)S(1)}, bf16[6,128,128]{2,1,0:T(8,128)(2,1)S(1)}, u32[]{:S(2)}, u32[]{:S(2)}) collective-permute-start(bf16[6,128,128]{2,1,0:T(8,128)(2,1)S(1)} %get-tuple-element.88), channel_id=1, source_target_pairs={{4,0},{5,1},{6,2},{7,3},{8,4},{9,5},{10,6},{11,7},{12,8},{13,9},{1... | collective-permute-start | bytes 589832 | tf_op jit(solution)/shard_map/ppermute | solution.py:209
  108.1 4.7 %inner_grads.7 = (bf16[1,384,4096]{2,1,0:T(8,128)(2,1)}, f32[384,512]{1,0:T(8,128)S(1)}, f32[384,512]{1,0:T(8,128)S(1)}) custom-call(s32[1]{0:T(128)} %bitcast.side_ref, bf16[1,384,4096]{2,1,0:T(8,128)(2,1)S(1)} %copy-done.3, bf16[1,384,4096]{2,1,0:T(8,128)(2,1)S(1)} %copy-done.1, ...), custom_call_target="tpu_custom_call", output_to_operand_aliasing={{0}: (8, {})} | custom-call | flops 553648128 | bytes 15728640 | tf_op jit(solution)/shard_map/inner_grads/pallas_call | solution.py:73
  112.9 1.1 collective-permute-done.16
  114.0 0.4 select_convert_fusion
  114.4 1.3 collective-permute-start.17
  115.7 3.0 %collective-permute-done.13 = bf16[6,128,128]{2,1,0:T(8,128)(2,1)S(1)} collective-permute-done((bf16[6,128,128]{2,1,0:T(8,128)(2,1)S(1)}, bf16[6,128,128]{2,1,0:T(8,128)(2,1)S(1)}, u32[]{:S(2)}, u32[]{:S(2)}) %collective-permute-start.13) | collective-permute-done | bytes 196640 | tf_op jit(solution)/shard_map/ppermute | solution.py:209
  118.7 0.2 fusion.13
  118.9 2.1 %collective-permute-start.15 = (bf16[6,128,128]{2,1,0:T(8,128)(2,1)S(1)}, bf16[6,128,128]{2,1,0:T(8,128)(2,1)S(1)}, u32[]{:S(2)}, u32[]{:S(2)}) collective-permute-start(bf16[6,128,128]{2,1,0:T(8,128)(2,1)S(1)} %fusion.13), channel_id=1, source_target_pairs={{0,2},{1,3},{2,0},{3,1},{4,6},{5,7},{6,4},{7,5},{8,10},{9,11},{10,... | collective-permute-start | bytes 589832 | tf_op jit(solution)/shard_map/ppermute | solution.py:209
  121.2 3.1 %finish_grads.4 = (bf16[1,384,4096]{2,1,0:T(8,128)(2,1)}, bf16[1,384,4096]{2,1,0:T(8,128)(2,1)}) custom-call(s32[1]{0:T(128)} %bitcast.side_ref, bf16[1,384,4096]{2,1,0:T(8,128)(2,1)S(1)} %copy-done.1, bf16[1,384,4096]{2,1,0:T(8,128)(2,1)S(1)} %copy-done.2, f32[384,1024]{1,0:T(8,128)S(1)} %copy-done.8, f32[384,1024]{1,0:T(8,128)S(1)} %copy-done.9, ...), custom_call_target="tpu_custom_call" | custom-call | flops 201326592 | bytes 11796480 | tf_op jit(solution)/shard_map/finish_grads/pallas_call | solution.py:73
  124.3 1.9 %collective-permute-done.15 = bf16[6,128,128]{2,1,0:T(8,128)(2,1)S(1)} collective-permute-done((bf16[6,128,128]{2,1,0:T(8,128)(2,1)S(1)}, bf16[6,128,128]{2,1,0:T(8,128)(2,1)S(1)}, u32[]{:S(2)}, u32[]{:S(2)}) %collective-permute-start.15) | collective-permute-done | bytes 196640 | tf_op jit(solution)/shard_map/ppermute | solution.py:209
  126.2 0.3 select_convert_fusion.2
  126.5 1.7 %collective-permute-start.18 = (bf16[6,128,128]{2,1,0:T(8,128)(2,1)S(1)}, bf16[6,128,128]{2,1,0:T(8,128)(2,1)S(1)}, u32[]{:S(2)}, u32[]{:S(2)}) collective-permute-start(bf16[6,128,128]{2,1,0:T(8,128)(2,1)S(1)} %get-tuple-element.94), channel_id=1, source_target_pairs={{0,1},{1,0},{2,3},{3,2},{4,5},{5,4},{6,7},{7,6},{8,9},{9,8},{10,11... | collective-permute-start | bytes 589832 | tf_op jit(solution)/shard_map/ppermute | solution.py:209
  128.2 4.4 %finish_grads.5 = (bf16[1,384,4096]{2,1,0:T(8,128)(2,1)}, bf16[1,384,4096]{2,1,0:T(8,128)(2,1)}) custom-call(s32[1]{0:T(128)} %bitcast.side_ref, bf16[1,384,4096]{2,1,0:T(8,128)(2,1)S(1)} %copy-done.1, bf16[1,384,4096]{2,1,0:T(8,128)(2,1)S(1)} %copy-done.2, f32[384,1536]{1,0:T(8,128)S(1)} %get-tuple-element.77.ki_ref, ...), custom_call_target="tpu_custom_call", output_to_operand_aliasing={{0}: (8, {}), {1}: (9, {})} | custom-call | flops 301989888 | bytes 17694720 | tf_op jit(solution)/shard_map/finish_grads/pallas_call | solution.py:73
  132.6 3.2 %finish_grads.6 = (bf16[1,384,4096]{2,1,0:T(8,128)(2,1)}, bf16[1,384,4096]{2,1,0:T(8,128)(2,1)}) custom-call(s32[1]{0:T(128)} %bitcast.side_ref, bf16[1,384,4096]{2,1,0:T(8,128)(2,1)S(1)} %copy-done.1, bf16[1,384,4096]{2,1,0:T(8,128)(2,1)S(1)} %copy-done.2, f32[384,1024]{1,0:T(8,128)S(1)} %copy-done.11, ...), custom_call_target="tpu_custom_call", output_to_operand_aliasing={{0}: (8, {}), {1}: (9, {})} | custom-call | flops 201326592 | bytes 11796480 | tf_op jit(solution)/shard_map/finish_grads/pallas_call | solution.py:73
  135.7 1.8 %finish_grads.7 = (bf16[1,384,4096]{2,1,0:T(8,128)(2,1)}, bf16[1,384,4096]{2,1,0:T(8,128)(2,1)}) custom-call(s32[1]{0:T(128)} %bitcast.side_ref, bf16[1,384,4096]{2,1,0:T(8,128)(2,1)S(1)} %copy-done.1, bf16[1,384,4096]{2,1,0:T(8,128)(2,1)S(1)} %copy-done.2, f32[384,512]{1,0:T(8,128)S(1)} %get-tuple-element.64.ki_ref, ...), custom_call_target="tpu_custom_call", output_to_operand_aliasing={{0}: (8, {}), {1}: (9, {})} | custom-call | flops 100663296 | bytes 5898240 | tf_op jit(solution)/shard_map/finish_grads/pallas_call | solution.py:73
  (71 shorter events, 1.7 us)
Async XLA Ops:
  0.6 23.5 %copy-start = (f32[1,32,384]{2,1,0:T(8,128)S(1)}, f32[1,32,384]{2,1,0:T(8,128)}, u32[]{:S(2)}) copy-start(f32[1,32,384]{2,1,0:T(8,128)} %param.11) | copy-start | bytes 147460
  0.6 26.6 %copy-start.14 = (bf16[1,384,4096]{2,1,0:T(8,128)(2,1)S(1)}, bf16[1,384,4096]{2,1,0:T(8,128)(2,1)}, u32[]{:S(2)}) copy-start(bf16[1,384,4096]{2,1,0:T(8,128)(2,1)} %param.10) | copy-start | bytes 9437188
  2.9 31.5 %collective-permute-start = (bf16[1,384,1024]{2,1,0:T(8,128)(2,1)}, bf16[1,384,1024]{2,1,0:T(8,128)(2,1)}, u32[]{:S(2)}, u32[]{:S(2)}) collective-permute-start(bf16[1,384,1024]{2,1,0:T(8,128)(2,1)} %slice.62), channel_id=1, source_target_pairs={{16,0},{32,16},{48,32},{64,48},{80,64},{96,80},{112,96},{0,112},{1... | collective-permute-start | bytes 2359304 | tf_op jit(solution)/shard_map/ppermute | solution.py:232
  9.5 22.0 %collective-permute-start.4 = (s32[1]{0:T(128)}, s32[1]{0:T(128)}, u32[]{:S(2)}, u32[]{:S(2)}) collective-permute-start(s32[1]{0:T(128)} %add.106), channel_id=1, source_target_pairs={{0,1},{1,2},{2,3},{3,4},{4,5},{5,6},{6,7},{7,8},{8,9},{9,10},{10,1... | collective-permute-start | bytes 20 | tf_op jit(solution)/shard_map/ppermute | solution.py:234
  34.4 28.4 %collective-permute-start.3 = (bf16[1,384,1536]{2,1,0:T(8,128)(2,1)}, bf16[1,384,1536]{2,1,0:T(8,128)(2,1)}, u32[]{:S(2)}, u32[]{:S(2)}) collective-permute-start(bf16[1,384,1536]{2,1,0:T(8,128)(2,1)} %slice.65), channel_id=1, source_target_pairs={{16,0},{32,16},{48,32},{64,48},{80,64},{96,80},{112,96},{0,112},{1... | collective-permute-start | bytes 3538952 | tf_op jit(solution)/shard_map/ppermute | solution.py:262
  34.4 65.4 %collective-permute-start.1 = (bf16[1,384,512]{2,1,0:T(8,128)(2,1)}, bf16[1,384,512]{2,1,0:T(8,128)(2,1)}, u32[]{:S(2)}, u32[]{:S(2)}) collective-permute-start(bf16[1,384,512]{2,1,0:T(8,128)(2,1)} %slice.63), channel_id=1, source_target_pairs={{16,0},{32,16},{48,32},{64,48},{80,64},{96,80},{112,96},{0,112},{1... | collective-permute-start | bytes 1179656 | tf_op jit(solution)/shard_map/ppermute | solution.py:262
  34.5 49.8 %collective-permute-start.2 = (bf16[1,384,1024]{2,1,0:T(8,128)(2,1)}, bf16[1,384,1024]{2,1,0:T(8,128)(2,1)}, u32[]{:S(2)}, u32[]{:S(2)}) collective-permute-start(bf16[1,384,1024]{2,1,0:T(8,128)(2,1)} %slice.64), channel_id=1, source_target_pairs={{16,0},{32,16},{48,32},{64,48},{80,64},{96,80},{112,96},{0,112},{1... | collective-permute-start | bytes 2359304 | tf_op jit(solution)/shard_map/ppermute | solution.py:262
  34.6 28.2 %copy-start.1 = (bf16[1,384,4096]{2,1,0:T(8,128)(2,1)S(1)}, bf16[1,384,4096]{2,1,0:T(8,128)(2,1)}, u32[]{:S(2)}) copy-start(bf16[1,384,4096]{2,1,0:T(8,128)(2,1)} %k_ref.15) | copy-start | bytes 9437188
  34.6 28.2 %copy-start.4 = (f32[1,1,32,128,128]{4,3,2,1,0:T(8,128)S(1)}, f32[1,1,32,128,128]{4,3,2,1,0:T(8,128)}, u32[]{:S(2)}) copy-start(f32[1,1,32,128,128]{4,3,2,1,0:T(8,128)} %p_ref.7) | copy-start | bytes 6291460
  34.6 28.2 %copy-start.5 = (f32[16,8,384]{2,1,0:T(8,128)S(1)}, f32[16,8,384]{2,1,0:T(8,128)}, u32[]{:S(2)}) copy-start(f32[16,8,384]{2,1,0:T(8,128)} %maximum_maximum_fusion.pack_ref) | copy-start | bytes 589828
  44.5 1.2 collective-permute-start.6
  45.7 33.4 %collective-permute-start.11 = (f32[32]{0:T(128)S(1)}, f32[32]{0:T(128)S(1)}, u32[]{:S(2)}, u32[]{:S(2)}) collective-permute-start(f32[32]{0:T(128)S(1)} %get-tuple-element.85), channel_id=1, source_target_pairs={{8,0},{9,1},{10,2},{11,3},{12,4},{13,5},{14,6},{15,7},{24,16},{25,... | collective-permute-start | bytes 392 | tf_op jit(solution)/shard_map/ppermute | solution.py:209
  47.0 32.1 %collective-permute-start.10 = (f32[32]{0:T(128)S(1)}, f32[32]{0:T(128)S(1)}, u32[]{:S(2)}, u32[]{:S(2)}) collective-permute-start(f32[32]{0:T(128)S(1)} %get-tuple-element.85), channel_id=1, source_target_pairs={{4,0},{5,1},{6,2},{7,3},{8,4},{9,5},{10,6},{11,7},{12,8},{13,9},{1... | collective-permute-start | bytes 392 | tf_op jit(solution)/shard_map/ppermute | solution.py:209
  62.8 1.9 %copy-start.3 = (bf16[1,384,4096]{2,1,0:T(8,128)(2,1)S(1)}, bf16[1,384,4096]{2,1,0:T(8,128)(2,1)}, u32[]{:S(2)}) copy-start(bf16[1,384,4096]{2,1,0:T(8,128)(2,1)} %q_ref.9) | copy-start | bytes 9437188
  64.7 1.1 copy-start.6
  78.6 9.2 %copy-start.2 = (bf16[1,384,4096]{2,1,0:T(8,128)(2,1)S(1)}, bf16[1,384,4096]{2,1,0:T(8,128)(2,1)}, u32[]{:S(2)}) copy-start(bf16[1,384,4096]{2,1,0:T(8,128)(2,1)} %v_ref.15) | copy-start | bytes 9437188
  78.7 5.7 %collective-permute-start.5 = (f32[10,128,128]{2,1,0:T(8,128)S(1)}, f32[10,128,128]{2,1,0:T(8,128)S(1)}, u32[]{:S(2)}, u32[]{:S(2)}) collective-permute-start(f32[10,128,128]{2,1,0:T(8,128)S(1)} %pad_maximum_fusion.1), channel_id=1, source_target_pairs={{0,1},{1,0},{2,3},{3,2},{4,5},{5,4},{6,7},{7,6},{8,9},{9,8},{10,11... | collective-permute-start | bytes 1966088 | tf_op jit(solution)/shard_map/ppermute | solution.py:209
  79.2 20.0 %collective-permute-start.12 = (f32[3,32]{1,0:T(4,128)S(1)}, f32[3,32]{1,0:T(4,128)S(1)}, u32[]{:S(2)}, u32[]{:S(2)}) collective-permute-start(f32[3,32]{1,0:T(4,128)S(1)} %pad_maximum_fusion.4), channel_id=1, source_target_pairs={{0,2},{1,3},{2,0},{3,1},{4,6},{5,7},{6,4},{7,5},{8,10},{9,11},{10,... | collective-permute-start | bytes 1160 | tf_op jit(solution)/shard_map/ppermute | solution.py:209
  84.6 17.8 %collective-permute-start.9 = (bf16[10,128,128]{2,1,0:T(8,128)(2,1)S(1)}, bf16[10,128,128]{2,1,0:T(8,128)(2,1)S(1)}, u32[]{:S(2)}, u32[]{:S(2)}) collective-permute-start(bf16[10,128,128]{2,1,0:T(8,128)(2,1)S(1)} %get-tuple-element.90), channel_id=1, source_target_pairs={{8,0},{9,1},{10,2},{11,3},{12,4},{13,5},{14,6},{15,7},{24,16},{25,... | collective-permute-start | bytes 983048 | tf_op jit(solution)/shard_map/ppermute | solution.py:209
  85.9 17.4 %collective-permute-start.8 = (bf16[10,128,128]{2,1,0:T(8,128)(2,1)S(1)}, bf16[10,128,128]{2,1,0:T(8,128)(2,1)S(1)}, u32[]{:S(2)}, u32[]{:S(2)}) collective-permute-start(bf16[10,128,128]{2,1,0:T(8,128)(2,1)S(1)} %get-tuple-element.90), channel_id=1, source_target_pairs={{4,0},{5,1},{6,2},{7,3},{8,4},{9,5},{10,6},{11,7},{12,8},{13,9},{1... | collective-permute-start | bytes 983048 | tf_op jit(solution)/shard_map/ppermute | solution.py:209
  96.9 1.2 copy-start.10
  98.0 1.1 copy-start.12
  101.9 6.3 %copy-start.7 = (f32[384,384]{1,0:T(8,128)S(1)}, f32[384,384]{1,0:T(8,128)}, u32[]{:S(2)}) copy-start(f32[384,384]{1,0:T(8,128)} %fusion.8.mask_ref) | copy-start | bytes 1769476
  101.9 2.6 %collective-permute-start.7 = (f32[6,128,128]{2,1,0:T(8,128)S(1)}, f32[6,128,128]{2,1,0:T(8,128)S(1)}, u32[]{:S(2)}, u32[]{:S(2)}) collective-permute-start(f32[6,128,128]{2,1,0:T(8,128)S(1)} %pad_maximum_fusion.3), channel_id=1, source_target_pairs={{0,1},{1,0},{2,3},{3,2},{4,5},{5,4},{6,7},{7,6},{8,9},{9,8},{10,11... | collective-permute-start | bytes 1179656 | tf_op jit(solution)/shard_map/ppermute | solution.py:209
  103.5 10.5 %collective-permute-start.16 = (bf16[10,128,128]{2,1,0:T(8,128)(2,1)S(1)}, bf16[10,128,128]{2,1,0:T(8,128)(2,1)S(1)}, u32[]{:S(2)}, u32[]{:S(2)}) collective-permute-start(bf16[10,128,128]{2,1,0:T(8,128)(2,1)S(1)} %fusion.3), channel_id=1, source_target_pairs={{0,2},{1,3},{2,0},{3,1},{4,6},{5,7},{6,4},{7,5},{8,10},{9,11},{10,... | collective-permute-start | bytes 983048 | tf_op jit(solution)/shard_map/ppermute | solution.py:209
  104.7 11.0 %collective-permute-start.14 = (bf16[6,128,128]{2,1,0:T(8,128)(2,1)S(1)}, bf16[6,128,128]{2,1,0:T(8,128)(2,1)S(1)}, u32[]{:S(2)}, u32[]{:S(2)}) collective-permute-start(bf16[6,128,128]{2,1,0:T(8,128)(2,1)S(1)} %get-tuple-element.88), channel_id=1, source_target_pairs={{8,0},{9,1},{10,2},{11,3},{12,4},{13,5},{14,6},{15,7},{24,16},{25,... | collective-permute-start | bytes 589832 | tf_op jit(solution)/shard_map/ppermute | solution.py:209
  106.0 12.7 %collective-permute-start.13 = (bf16[6,128,128]{2,1,0:T(8,128)(2,1)S(1)}, bf16[6,128,128]{2,1,0:T(8,128)(2,1)S(1)}, u32[]{:S(2)}, u32[]{:S(2)}) collective-permute-start(bf16[6,128,128]{2,1,0:T(8,128)(2,1)S(1)} %get-tuple-element.88), channel_id=1, source_target_pairs={{4,0},{5,1},{6,2},{7,3},{8,4},{9,5},{10,6},{11,7},{12,8},{13,9},{1... | collective-permute-start | bytes 589832 | tf_op jit(solution)/shard_map/ppermute | solution.py:209
  112.8 8.3 %copy-start.8 = (f32[384,1024]{1,0:T(8,128)S(1)}, f32[384,1024]{1,0:T(8,128)}, u32[]{:S(2)}) copy-start(f32[384,1024]{1,0:T(8,128)} %get-tuple-element.68.ki_ref) | copy-start | bytes 4718596
  112.8 8.3 %copy-start.9 = (f32[384,1024]{1,0:T(8,128)S(1)}, f32[384,1024]{1,0:T(8,128)}, u32[]{:S(2)}) copy-start(f32[384,1024]{1,0:T(8,128)} %get-tuple-element.69.vi_ref) | copy-start | bytes 4718596
  114.4 6.8 %collective-permute-start.17 = (bf16[10,128,128]{2,1,0:T(8,128)(2,1)S(1)}, bf16[10,128,128]{2,1,0:T(8,128)(2,1)S(1)}, u32[]{:S(2)}, u32[]{:S(2)}) collective-permute-start(bf16[10,128,128]{2,1,0:T(8,128)(2,1)S(1)} %get-tuple-element.92), channel_id=1, source_target_pairs={{0,1},{1,0},{2,3},{3,2},{4,5},{5,4},{6,7},{7,6},{8,9},{9,8},{10,11... | collective-permute-start | bytes 983048 | tf_op jit(solution)/shard_map/ppermute | solution.py:209
  118.9 7.3 %collective-permute-start.15 = (bf16[6,128,128]{2,1,0:T(8,128)(2,1)S(1)}, bf16[6,128,128]{2,1,0:T(8,128)(2,1)S(1)}, u32[]{:S(2)}, u32[]{:S(2)}) collective-permute-start(bf16[6,128,128]{2,1,0:T(8,128)(2,1)S(1)} %fusion.13), channel_id=1, source_target_pairs={{0,2},{1,3},{2,0},{3,1},{4,6},{5,7},{6,4},{7,5},{8,10},{9,11},{10,... | collective-permute-start | bytes 589832 | tf_op jit(solution)/shard_map/ppermute | solution.py:209
  126.5 6.0 %collective-permute-start.18 = (bf16[6,128,128]{2,1,0:T(8,128)(2,1)S(1)}, bf16[6,128,128]{2,1,0:T(8,128)(2,1)S(1)}, u32[]{:S(2)}, u32[]{:S(2)}) collective-permute-start(bf16[6,128,128]{2,1,0:T(8,128)(2,1)S(1)} %get-tuple-element.94), channel_id=1, source_target_pairs={{0,1},{1,0},{2,3},{3,2},{4,5},{5,4},{6,7},{7,6},{8,9},{9,8},{10,11... | collective-permute-start | bytes 589832 | tf_op jit(solution)/shard_map/ppermute | solution.py:209
  128.2 4.4 %copy-start.11 = (f32[384,1024]{1,0:T(8,128)S(1)}, f32[384,1024]{1,0:T(8,128)}, u32[]{:S(2)}) copy-start(f32[384,1024]{1,0:T(8,128)} %copy-done.10) | copy-start | bytes 4718596
  128.2 4.4 %copy-start.13 = (f32[384,1024]{1,0:T(8,128)S(1)}, f32[384,1024]{1,0:T(8,128)}, u32[]{:S(2)}) copy-start(f32[384,1024]{1,0:T(8,128)} %copy-done.12) | copy-start | bytes 4718596

commit v3 on v2

--- a/solution.py
+++ b/solution.py
@@ -259,7 +259,8 @@
 
     for start, size in list(zip(starts, CHUNKS))[1:]:
         part = lax.slice_in_dim(after(next_grads, running), start * D, (start + size) * D, axis=2)
-        grads.append(lax.ppermute(after(part, grads[0]), "pipe", back))
+        ready = part if len(grads) == 1 else after(part, grads[0])
+        grads.append(lax.ppermute(ready, "pipe", back))
 
     def halves(table, members):
         return jnp.concatenate([part_of(table, starts[n] + side * (CHUNKS[n] // 2), CHUNKS[n] // 2) for n in members])

time: 138 us -> 130 us (0.942)
  waiting for transfers between devices: 23 us -> 12.7 us
  local copies, waits for them, and re-layouts: 14.6 us -> 16.6 us
    ppermute x3, waiting for transfers between devices: 16 us -> 4.45 us  [on_device(): grads.append(lax.ppermute(ready, 'pipe', back))]
    slice x3, local copies, waits for them, and re-layouts: 3.89 us -> 6.24 us  [on_device(): lax.slice_in_dim(after(next_grads, running), start * D, (start + size) *...]
  transfers between devices with their start and end apart: 19 -> 19, of which waited for: 6 -> 6; matrix products, arithmetic and copies ran while one was open for 10% -> 12% of each run, Pallas kernels for 33% -> 36%
where the time goes in v3:
time: 130 us; the launch traced here: 129 us
  Pallas kernels  51 us (39%)
  starting transfers between devices  38.2 us (29%)
  local copies, waits for them, and re-layouts  16.6 us (13%)
  waiting for transfers between devices  12.7 us (10%)
  other arithmetic  6.09 us (5%)
  between operations  4.26 us (3%)
    pallas_call x9, Pallas kernels, call(): pl.pallas_call(kernel, out_shape=tuple(out_shapes), grid_spec=pltpu.Prefe...  51 us
    ppermute x14, starting transfers between devices, moved(): return lax.ppermute(value, 'ctx', pairs)  19 us
    ppermute x1, starting transfers between devices, on_device(): lax.ppermute(docs[-1:] + 1, 'ctx', [(i, i + 1) for i in range(ctx - 1)])[0]  14.3 us
    ppermute x14, waiting for transfers between devices, moved(): return lax.ppermute(value, 'ctx', pairs)  8.29 us
    slice x3, local copies, waits for them, and re-layouts, on_device(): lax.slice_in_dim(after(next_grads, running), start * D, (start + size) *...  6.24 us
    unnamed x30, local copies, waits for them, and re-layouts  6.04 us
    ppermute x1, starting transfers between devices, on_device(): grads = [lax.ppermute(opening, 'pipe', back)]  4.75 us
    ppermute x3, waiting for transfers between devices, on_device(): grads.append(lax.ppermute(ready, 'pipe', back))  4.45 us
  transfers between devices with their start and end apart: 19, of which 6 were waited for; matrix products, arithmetic and copies ran while one was open for 12% of the time, Pallas kernels for 36%

profile of v3, /device:TPU:9, one launch (start us, length us, event | category | flops | bytes accessed | tf_op | source)
XLA Modules:
  0.0 129.3 jit_solution(3242183677419686012)
XLA Ops:
  0.6 1.2 slice.62
  1.8 4.8 %collective-permute-start = (bf16[1,384,1024]{2,1,0:T(8,128)(2,1)S(1)}, bf16[1,384,1024]{2,1,0:T(8,128)(2,1)S(1)}, u32[]{:S(2)}, u32[]{:S(2)}) collective-permute-start(bf16[1,384,1024]{2,1,0:T(8,128)(2,1)S(1)} %slice.62), channel_id=1, source_target_pairs={{16,0},{32,16},{48,32},{64,48},{80,64},{96,80},{112,96},{0,112},{1... | collective-permute-start | bytes 2359304 | tf_op jit(solution)/shard_map/ppermute | solution.py:232
  6.6 0.7 reduce
  7.3 0.6 fusion.28
  8.5 14.3 %collective-permute-start.4 = (s32[1]{0:T(128)}, s32[1]{0:T(128)}, u32[]{:S(2)}, u32[]{:S(2)}) collective-permute-start(s32[1]{0:T(128)} %add.106), channel_id=1, source_target_pairs={{0,1},{1,2},{2,3},{3,4},{4,5},{5,6},{6,7},{7,8},{8,9},{9,10},{10,1... | collective-permute-start | bytes 20 | tf_op jit(solution)/shard_map/ppermute | solution.py:234
  22.9 0.3 fusion.5
  23.2 2.4 %slice.65 = bf16[1,384,1536]{2,1,0:T(8,128)(2,1)} slice(bf16[1,384,4096]{2,1,0:T(8,128)(2,1)} %param.10), slice={[0:1], [0:384], [1024:2560]} | slice | bytes 2359296 | tf_op jit(solution)/shard_map/slice | solution.py:261
  25.6 0.2 slice_reduce_fusion
  25.8 1.8 %slice.63 = bf16[1,384,512]{2,1,0:T(8,128)(2,1)} slice(bf16[1,384,4096]{2,1,0:T(8,128)(2,1)} %param.10), slice={[0:1], [0:384], [3584:4096]} | slice | bytes 786432 | tf_op jit(solution)/shard_map/slice | solution.py:261
  27.6 0.9 fusion.8.mask_ref
  28.5 2.1 %slice.64 = bf16[1,384,1024]{2,1,0:T(8,128)(2,1)} slice(bf16[1,384,4096]{2,1,0:T(8,128)(2,1)} %param.10), slice={[0:1], [0:384], [2560:3584]} | slice | bytes 1572864 | tf_op jit(solution)/shard_map/slice | solution.py:261
  33.3 1.3 %and_select_fusion = (f32[384]{0:T(512)S(1)}, f32[384]{0:T(512)S(1)}) fusion(s32[384]{0:T(512)S(1)} %reduce, s32[]{:T(128)} %bitcast.2, pred[]{:T(512)S(6)} %eq.45, s32[]{:T(128)} %bitcast.4), kind=kLoop, calls=%fused_computation.48 | loop fusion | flops 1920 | bytes 4617 | tf_op jit(solution)/shard_map/jit(_where)/select_n | solution.py:248
  34.6 0.1 exponential_multiply_fusion.1
  34.8 0.8 maximum_maximum_fusion.pack_ref
  35.6 0.1 collective-permute-start.1
  35.7 0.1 collective-permute-start.2
  35.7 0.7 copy-done.14
  36.5 9.9 %inner_grads.4 = (bf16[1,384,4096]{2,1,0:T(8,128)(2,1)}, f32[384,1024]{1,0:T(8,128)}, f32[384,1024]{1,0:T(8,128)}, f32[8,128,128]{2,1,0:T(8,128)}) custom-call(s32[1]{0:T(128)} %bitcast.side_ref, bf16[1,384,4096]{2,1,0:T(8,128)(2,1)} %q_ref.9, bf16[1,384,4096]{2,1,0:T(8,128)(2,1)} %k_ref.15, bf16[1,384,4096]{2,1,0:T(8,128)(2,1)} %v_ref.15, ...), custom_call_target="tpu_custom_call" | custom-call | flops 1107296256 | bytes 31457280 | tf_op jit(solution)/shard_map/inner_grads/pallas_call | solution.py:73
  46.4 0.1 collective-permute-start.6
  46.5 1.1 fusion.26
  47.6 1.3 collective-permute-start.11
  48.9 2.1 %collective-permute-start.10 = (f32[32]{0:T(128)S(1)}, f32[32]{0:T(128)S(1)}, u32[]{:S(2)}, u32[]{:S(2)}) collective-permute-start(f32[32]{0:T(128)S(1)} %get-tuple-element.83), channel_id=1, source_target_pairs={{4,0},{5,1},{6,2},{7,3},{8,4},{9,5},{10,6},{11,7},{12,8},{13,9},{1... | collective-permute-start | bytes 392 | tf_op jit(solution)/shard_map/ppermute | solution.py:209
  51.0 0.1 dynamic-slice_bitcast_fusion.6
  51.2 0.1 dynamic-slice_bitcast_fusion.15
  51.3 2.7 %collective-permute-done.3.g_ref = bf16[1,384,1536]{2,1,0:T(8,128)(2,1)} collective-permute-done((bf16[1,384,1536]{2,1,0:T(8,128)(2,1)}, bf16[1,384,1536]{2,1,0:T(8,128)(2,1)}, u32[]{:S(2)}, u32[]{:S(2)}) %collective-permute-start.3) | collective-permute-done | bytes 1179680 | tf_op jit(solution)/shard_map/ppermute | solution.py:263
  54.0 1.9 %copy-done.3 = bf16[1,384,4096]{2,1,0:T(8,128)(2,1)S(1)} copy-done((bf16[1,384,4096]{2,1,0:T(8,128)(2,1)S(1)}, bf16[1,384,4096]{2,1,0:T(8,128)(2,1)}, u32[]{:S(2)}) %copy-start.3) | copy-done | bytes 3145752
  55.9 1.1 copy-done.6
  56.9 12.8 %inner_grads.5 = (bf16[1,384,4096]{2,1,0:T(8,128)(2,1)}, f32[384,1536]{1,0:T(8,128)S(1)}, f32[384,1536]{1,0:T(8,128)S(1)}, f32[12,128,128]{2,1,0:T(8,128)S(1)}) custom-call(s32[1]{0:T(128)} %bitcast.side_ref, bf16[1,384,4096]{2,1,0:T(8,128)(2,1)S(1)} %copy-done.3, bf16[1,384,4096]{2,1,0:T(8,128)(2,1)S(1)} %copy-done.1, ...), custom_call_target="tpu_custom_call", output_to_operand_aliasing={{0}: (8, {})} | custom-call | flops 1660944384 | bytes 47185920 | tf_op jit(solution)/shard_map/inner_grads/pallas_call | solution.py:73
  69.9 0.1 collective-permute-start.5
  70.0 0.1 dynamic-slice_bitcast_fusion.16
  70.0 0.1 maximum_bitcast_fusion.1
  70.4 2.5 %collective-permute-start.12 = (f32[3,32]{1,0:T(4,128)S(1)}, f32[3,32]{1,0:T(4,128)S(1)}, u32[]{:S(2)}, u32[]{:S(2)}) collective-permute-start(f32[3,32]{1,0:T(4,128)S(1)} %pad_maximum_fusion.4), channel_id=1, source_target_pairs={{0,2},{1,3},{2,0},{3,1},{4,6},{5,7},{6,4},{7,5},{8,10},{9,11},{10,... | collective-permute-start | bytes 1160 | tf_op jit(solution)/shard_map/ppermute | solution.py:209
  72.9 1.7 %collective-permute-done.2.g_ref = bf16[1,384,1024]{2,1,0:T(8,128)(2,1)} collective-permute-done((bf16[1,384,1024]{2,1,0:T(8,128)(2,1)}, bf16[1,384,1024]{2,1,0:T(8,128)(2,1)}, u32[]{:S(2)}, u32[]{:S(2)}) %collective-permute-start.2) | collective-permute-done | bytes 786464 | tf_op jit(solution)/shard_map/ppermute | solution.py:263
  74.6 0.2 fusion.23
  74.8 1.3 collective-permute-start.9
  76.1 2.1 %collective-permute-start.8 = (bf16[10,128,128]{2,1,0:T(8,128)(2,1)S(1)}, bf16[10,128,128]{2,1,0:T(8,128)(2,1)S(1)}, u32[]{:S(2)}, u32[]{:S(2)}) collective-permute-start(bf16[10,128,128]{2,1,0:T(8,128)(2,1)S(1)} %get-tuple-element.88), channel_id=1, source_target_pairs={{4,0},{5,1},{6,2},{7,3},{8,4},{9,5},{10,6},{11,7},{12,8},{13,9},{1... | collective-permute-start | bytes 983048 | tf_op jit(solution)/shard_map/ppermute | solution.py:209
  78.2 9.1 %inner_grads.6 = (bf16[1,384,4096]{2,1,0:T(8,128)(2,1)}, f32[384,1024]{1,0:T(8,128)S(1)}, f32[384,1024]{1,0:T(8,128)S(1)}, f32[8,128,128]{2,1,0:T(8,128)S(1)}) custom-call(s32[1]{0:T(128)} %bitcast.side_ref, bf16[1,384,4096]{2,1,0:T(8,128)(2,1)S(1)} %copy-done.3, bf16[1,384,4096]{2,1,0:T(8,128)(2,1)S(1)} %copy-done.1, ...), custom_call_target="tpu_custom_call", output_to_operand_aliasing={{0}: (8, {})} | custom-call | flops 1107296256 | bytes 31457280 | tf_op jit(solution)/shard_map/inner_grads/pallas_call | solution.py:73
  87.3 1.2 copy-done.10
  88.5 1.1 copy-done.12
  89.7 0.1 dynamic-slice_bitcast_fusion.4
  90.0 0.1 dynamic-slice_bitcast_fusion.1
  90.3 2.0 %head_states.1 = f32[4,128,128]{2,1,0:T(8,128)S(1)} custom-call(s32[1]{0:T(128)} %bitcast.side_ref, bf16[1,384,4096]{2,1,0:T(8,128)(2,1)S(1)} %copy-done.3, bf16[1,384,512]{2,1,0:T(8,128)(2,1)} %collective-permute-done.1.g_ref, f32[16,8,384]{2,1,0:T(8,128)S(1)} %copy-done.5), custom_call_target="tpu_custom_call" | custom-call | flops 50331648 | bytes 5111808 | tf_op jit(solution)/shard_map/head_states/pallas_call | solution.py:73
  92.4 0.1 collective-permute-start.7
  92.7 0.1 maximum_bitcast_fusion.7
  92.8 1.6 %collective-permute-done.8 = bf16[10,128,128]{2,1,0:T(8,128)(2,1)S(1)} collective-permute-done((bf16[10,128,128]{2,1,0:T(8,128)(2,1)S(1)}, bf16[10,128,128]{2,1,0:T(8,128)(2,1)S(1)}, u32[]{:S(2)}, u32[]{:S(2)}) %collective-permute-start.8) | collective-permute-done | bytes 327712 | tf_op jit(solution)/shard_map/ppermute | solution.py:209
  94.4 0.3 fusion.3
  94.7 1.6 %collective-permute-start.16 = (bf16[10,128,128]{2,1,0:T(8,128)(2,1)S(1)}, bf16[10,128,128]{2,1,0:T(8,128)(2,1)S(1)}, u32[]{:S(2)}, u32[]{:S(2)}) collective-permute-start(bf16[10,128,128]{2,1,0:T(8,128)(2,1)S(1)} %fusion.3), channel_id=1, source_target_pairs={{0,2},{1,3},{2,0},{3,1},{4,6},{5,7},{6,4},{7,5},{8,10},{9,11},{10,... | collective-permute-start | bytes 983048 | tf_op jit(solution)/shard_map/ppermute | solution.py:209
  96.3 0.1 fusion.22
  96.5 1.3 collective-permute-start.14
  97.8 2.1 %collective-permute-start.13 = (bf16[6,128,128]{2,1,0:T(8,128)(2,1)S(1)}, bf16[6,128,128]{2,1,0:T(8,128)(2,1)S(1)}, u32[]{:S(2)}, u32[]{:S(2)}) collective-permute-start(bf16[6,128,128]{2,1,0:T(8,128)(2,1)S(1)} %get-tuple-element.86), channel_id=1, source_target_pairs={{4,0},{5,1},{6,2},{7,3},{8,4},{9,5},{10,6},{11,7},{12,8},{13,9},{1... | collective-permute-start | bytes 589832 | tf_op jit(solution)/shard_map/ppermute | solution.py:209
  99.9 4.7 %inner_grads.7 = (bf16[1,384,4096]{2,1,0:T(8,128)(2,1)}, f32[384,512]{1,0:T(8,128)S(1)}, f32[384,512]{1,0:T(8,128)S(1)}) custom-call(s32[1]{0:T(128)} %bitcast.side_ref, bf16[1,384,4096]{2,1,0:T(8,128)(2,1)S(1)} %copy-done.3, bf16[1,384,4096]{2,1,0:T(8,128)(2,1)S(1)} %copy-done.1, ...), custom_call_target="tpu_custom_call", output_to_operand_aliasing={{0}: (8, {})} | custom-call | flops 553648128 | bytes 15728640 | tf_op jit(solution)/shard_map/inner_grads/pallas_call | solution.py:73
  104.6 0.6 collective-permute-done.16
  105.2 0.4 select_convert_fusion
  105.6 1.3 %collective-permute-start.17 = (bf16[10,128,128]{2,1,0:T(8,128)(2,1)S(1)}, bf16[10,128,128]{2,1,0:T(8,128)(2,1)S(1)}, u32[]{:S(2)}, u32[]{:S(2)}) collective-permute-start(bf16[10,128,128]{2,1,0:T(8,128)(2,1)S(1)} %get-tuple-element.90), channel_id=1, source_target_pairs={{0,1},{1,0},{2,3},{3,2},{4,5},{5,4},{6,7},{7,6},{8,9},{9,8},{10,11... | collective-permute-start | bytes 983048 | tf_op jit(solution)/shard_map/ppermute | solution.py:209
  106.9 3.6 %collective-permute-done.13 = bf16[6,128,128]{2,1,0:T(8,128)(2,1)S(1)} collective-permute-done((bf16[6,128,128]{2,1,0:T(8,128)(2,1)S(1)}, bf16[6,128,128]{2,1,0:T(8,128)(2,1)S(1)}, u32[]{:S(2)}, u32[]{:S(2)}) %collective-permute-start.13) | collective-permute-done | bytes 196640 | tf_op jit(solution)/shard_map/ppermute | solution.py:209
  110.5 0.2 fusion.13
  110.7 1.6 %collective-permute-start.15 = (bf16[6,128,128]{2,1,0:T(8,128)(2,1)S(1)}, bf16[6,128,128]{2,1,0:T(8,128)(2,1)S(1)}, u32[]{:S(2)}, u32[]{:S(2)}) collective-permute-start(bf16[6,128,128]{2,1,0:T(8,128)(2,1)S(1)} %fusion.13), channel_id=1, source_target_pairs={{0,2},{1,3},{2,0},{3,1},{4,6},{5,7},{6,4},{7,5},{8,10},{9,11},{10,... | collective-permute-start | bytes 589832 | tf_op jit(solution)/shard_map/ppermute | solution.py:209
  112.4 3.1 %finish_grads.4 = (bf16[1,384,4096]{2,1,0:T(8,128)(2,1)}, bf16[1,384,4096]{2,1,0:T(8,128)(2,1)}) custom-call(s32[1]{0:T(128)} %bitcast.side_ref, bf16[1,384,4096]{2,1,0:T(8,128)(2,1)S(1)} %copy-done.1, bf16[1,384,4096]{2,1,0:T(8,128)(2,1)S(1)} %copy-done.2, f32[384,1024]{1,0:T(8,128)S(1)} %copy-done.8, f32[384,1024]{1,0:T(8,128)S(1)} %copy-done.9, ...), custom_call_target="tpu_custom_call" | custom-call | flops 201326592 | bytes 11796480 | tf_op jit(solution)/shard_map/finish_grads/pallas_call | solution.py:73
  115.5 2.4 %collective-permute-done.15 = bf16[6,128,128]{2,1,0:T(8,128)(2,1)S(1)} collective-permute-done((bf16[6,128,128]{2,1,0:T(8,128)(2,1)S(1)}, bf16[6,128,128]{2,1,0:T(8,128)(2,1)S(1)}, u32[]{:S(2)}, u32[]{:S(2)}) %collective-permute-start.15) | collective-permute-done | bytes 196640 | tf_op jit(solution)/shard_map/ppermute | solution.py:209
  118.0 0.3 select_convert_fusion.2
  118.3 1.7 %collective-permute-start.18 = (bf16[6,128,128]{2,1,0:T(8,128)(2,1)S(1)}, bf16[6,128,128]{2,1,0:T(8,128)(2,1)S(1)}, u32[]{:S(2)}, u32[]{:S(2)}) collective-permute-start(bf16[6,128,128]{2,1,0:T(8,128)(2,1)S(1)} %get-tuple-element.92), channel_id=1, source_target_pairs={{0,1},{1,0},{2,3},{3,2},{4,5},{5,4},{6,7},{7,6},{8,9},{9,8},{10,11... | collective-permute-start | bytes 589832 | tf_op jit(solution)/shard_map/ppermute | solution.py:209
  119.9 4.4 %finish_grads.5 = (bf16[1,384,4096]{2,1,0:T(8,128)(2,1)}, bf16[1,384,4096]{2,1,0:T(8,128)(2,1)}) custom-call(s32[1]{0:T(128)} %bitcast.side_ref, bf16[1,384,4096]{2,1,0:T(8,128)(2,1)S(1)} %copy-done.1, bf16[1,384,4096]{2,1,0:T(8,128)(2,1)S(1)} %copy-done.2, f32[384,1536]{1,0:T(8,128)S(1)} %get-tuple-element.75.ki_ref, ...), custom_call_target="tpu_custom_call", output_to_operand_aliasing={{0}: (8, {}), {1}: (9, {})} | custom-call | flops 301989888 | bytes 17694720 | tf_op jit(solution)/shard_map/finish_grads/pallas_call | solution.py:73
  124.3 3.2 %finish_grads.6 = (bf16[1,384,4096]{2,1,0:T(8,128)(2,1)}, bf16[1,384,4096]{2,1,0:T(8,128)(2,1)}) custom-call(s32[1]{0:T(128)} %bitcast.side_ref, bf16[1,384,4096]{2,1,0:T(8,128)(2,1)S(1)} %copy-done.1, bf16[1,384,4096]{2,1,0:T(8,128)(2,1)S(1)} %copy-done.2, f32[384,1024]{1,0:T(8,128)S(1)} %copy-done.11, ...), custom_call_target="tpu_custom_call", output_to_operand_aliasing={{0}: (8, {}), {1}: (9, {})} | custom-call | flops 201326592 | bytes 11796480 | tf_op jit(solution)/shard_map/finish_grads/pallas_call | solution.py:73
  127.5 1.8 %finish_grads.7 = (bf16[1,384,4096]{2,1,0:T(8,128)(2,1)}, bf16[1,384,4096]{2,1,0:T(8,128)(2,1)}) custom-call(s32[1]{0:T(128)} %bitcast.side_ref, bf16[1,384,4096]{2,1,0:T(8,128)(2,1)S(1)} %copy-done.1, bf16[1,384,4096]{2,1,0:T(8,128)(2,1)S(1)} %copy-done.2, f32[384,512]{1,0:T(8,128)S(1)} %get-tuple-element.62.ki_ref, ...), custom_call_target="tpu_custom_call", output_to_operand_aliasing={{0}: (8, {}), {1}: (9, {})} | custom-call | flops 100663296 | bytes 5898240 | tf_op jit(solution)/shard_map/finish_grads/pallas_call | solution.py:73
  (71 shorter events, 1.8 us)
Async XLA Ops:
  0.6 22.2 %copy-start = (f32[1,32,384]{2,1,0:T(8,128)S(1)}, f32[1,32,384]{2,1,0:T(8,128)}, u32[]{:S(2)}) copy-start(f32[1,32,384]{2,1,0:T(8,128)} %param.11) | copy-start | bytes 147460
  1.8 33.7 %collective-permute-start = (bf16[1,384,1024]{2,1,0:T(8,128)(2,1)S(1)}, bf16[1,384,1024]{2,1,0:T(8,128)(2,1)S(1)}, u32[]{:S(2)}, u32[]{:S(2)}) collective-permute-start(bf16[1,384,1024]{2,1,0:T(8,128)(2,1)S(1)} %slice.62), channel_id=1, source_target_pairs={{16,0},{32,16},{48,32},{64,48},{80,64},{96,80},{112,96},{0,112},{1... | collective-permute-start | bytes 2359304 | tf_op jit(solution)/shard_map/ppermute | solution.py:232
  8.5 24.1 %collective-permute-start.4 = (s32[1]{0:T(128)}, s32[1]{0:T(128)}, u32[]{:S(2)}, u32[]{:S(2)}) collective-permute-start(s32[1]{0:T(128)} %add.106), channel_id=1, source_target_pairs={{0,1},{1,2},{2,3},{3,4},{4,5},{5,6},{6,7},{7,8},{8,9},{9,10},{10,1... | collective-permute-start | bytes 20 | tf_op jit(solution)/shard_map/ppermute | solution.py:234
  25.6 28.4 %collective-permute-start.3 = (bf16[1,384,1536]{2,1,0:T(8,128)(2,1)}, bf16[1,384,1536]{2,1,0:T(8,128)(2,1)}, u32[]{:S(2)}, u32[]{:S(2)}) collective-permute-start(bf16[1,384,1536]{2,1,0:T(8,128)(2,1)} %slice.65), channel_id=1, source_target_pairs={{16,0},{32,16},{48,32},{64,48},{80,64},{96,80},{112,96},{0,112},{1... | collective-permute-start | bytes 3538952 | tf_op jit(solution)/shard_map/ppermute | solution.py:263
  35.6 0.9 copy-start.14
  35.6 54.7 %collective-permute-start.1 = (bf16[1,384,512]{2,1,0:T(8,128)(2,1)}, bf16[1,384,512]{2,1,0:T(8,128)(2,1)}, u32[]{:S(2)}, u32[]{:S(2)}) collective-permute-start(bf16[1,384,512]{2,1,0:T(8,128)(2,1)} %slice.63), channel_id=1, source_target_pairs={{16,0},{32,16},{48,32},{64,48},{80,64},{96,80},{112,96},{0,112},{1... | collective-permute-start | bytes 1179656 | tf_op jit(solution)/shard_map/ppermute | solution.py:263
  35.7 39.0 %collective-permute-start.2 = (bf16[1,384,1024]{2,1,0:T(8,128)(2,1)}, bf16[1,384,1024]{2,1,0:T(8,128)(2,1)}, u32[]{:S(2)}, u32[]{:S(2)}) collective-permute-start(bf16[1,384,1024]{2,1,0:T(8,128)(2,1)} %slice.64), channel_id=1, source_target_pairs={{16,0},{32,16},{48,32},{64,48},{80,64},{96,80},{112,96},{0,112},{1... | collective-permute-start | bytes 2359304 | tf_op jit(solution)/shard_map/ppermute | solution.py:263
  36.5 17.5 %copy-start.1 = (bf16[1,384,4096]{2,1,0:T(8,128)(2,1)S(1)}, bf16[1,384,4096]{2,1,0:T(8,128)(2,1)}, u32[]{:S(2)}) copy-start(bf16[1,384,4096]{2,1,0:T(8,128)(2,1)} %k_ref.15) | copy-start | bytes 9437188
  36.5 17.5 %copy-start.4 = (f32[1,1,32,128,128]{4,3,2,1,0:T(8,128)S(1)}, f32[1,1,32,128,128]{4,3,2,1,0:T(8,128)}, u32[]{:S(2)}) copy-start(f32[1,1,32,128,128]{4,3,2,1,0:T(8,128)} %p_ref.7) | copy-start | bytes 6291460
  36.5 17.5 %copy-start.5 = (f32[16,8,384]{2,1,0:T(8,128)S(1)}, f32[16,8,384]{2,1,0:T(8,128)}, u32[]{:S(2)}) copy-start(f32[16,8,384]{2,1,0:T(8,128)} %maximum_maximum_fusion.pack_ref) | copy-start | bytes 589828
  46.4 1.2 collective-permute-start.6
  47.6 22.8 %collective-permute-start.11 = (f32[32]{0:T(128)S(1)}, f32[32]{0:T(128)S(1)}, u32[]{:S(2)}, u32[]{:S(2)}) collective-permute-start(f32[32]{0:T(128)S(1)} %get-tuple-element.83), channel_id=1, source_target_pairs={{8,0},{9,1},{10,2},{11,3},{12,4},{13,5},{14,6},{15,7},{24,16},{25,... | collective-permute-start | bytes 392 | tf_op jit(solution)/shard_map/ppermute | solution.py:209
  48.9 21.5 %collective-permute-start.10 = (f32[32]{0:T(128)S(1)}, f32[32]{0:T(128)S(1)}, u32[]{:S(2)}, u32[]{:S(2)}) collective-permute-start(f32[32]{0:T(128)S(1)} %get-tuple-element.83), channel_id=1, source_target_pairs={{4,0},{5,1},{6,2},{7,3},{8,4},{9,5},{10,6},{11,7},{12,8},{13,9},{1... | collective-permute-start | bytes 392 | tf_op jit(solution)/shard_map/ppermute | solution.py:209
  54.0 1.9 %copy-start.3 = (bf16[1,384,4096]{2,1,0:T(8,128)(2,1)S(1)}, bf16[1,384,4096]{2,1,0:T(8,128)(2,1)}, u32[]{:S(2)}) copy-start(bf16[1,384,4096]{2,1,0:T(8,128)(2,1)} %q_ref.9) | copy-start | bytes 9437188
  55.9 1.1 copy-start.6
  69.8 8.5 %copy-start.2 = (bf16[1,384,4096]{2,1,0:T(8,128)(2,1)S(1)}, bf16[1,384,4096]{2,1,0:T(8,128)(2,1)}, u32[]{:S(2)}) copy-start(bf16[1,384,4096]{2,1,0:T(8,128)(2,1)} %v_ref.15) | copy-start | bytes 9437188
  69.9 4.8 %collective-permute-start.5 = (f32[10,128,128]{2,1,0:T(8,128)S(1)}, f32[10,128,128]{2,1,0:T(8,128)S(1)}, u32[]{:S(2)}, u32[]{:S(2)}) collective-permute-start(f32[10,128,128]{2,1,0:T(8,128)S(1)} %pad_maximum_fusion.1), channel_id=1, source_target_pairs={{0,1},{1,0},{2,3},{3,2},{4,5},{5,4},{6,7},{7,6},{8,9},{9,8},{10,11... | collective-permute-start | bytes 1966088 | tf_op jit(solution)/shard_map/ppermute | solution.py:209
  70.4 19.3 %collective-permute-start.12 = (f32[3,32]{1,0:T(4,128)S(1)}, f32[3,32]{1,0:T(4,128)S(1)}, u32[]{:S(2)}, u32[]{:S(2)}) collective-permute-start(f32[3,32]{1,0:T(4,128)S(1)} %pad_maximum_fusion.4), channel_id=1, source_target_pairs={{0,2},{1,3},{2,0},{3,1},{4,6},{5,7},{6,4},{7,5},{8,10},{9,11},{10,... | collective-permute-start | bytes 1160 | tf_op jit(solution)/shard_map/ppermute | solution.py:209
  74.8 17.9 %collective-permute-start.9 = (bf16[10,128,128]{2,1,0:T(8,128)(2,1)S(1)}, bf16[10,128,128]{2,1,0:T(8,128)(2,1)S(1)}, u32[]{:S(2)}, u32[]{:S(2)}) collective-permute-start(bf16[10,128,128]{2,1,0:T(8,128)(2,1)S(1)} %get-tuple-element.88), channel_id=1, source_target_pairs={{8,0},{9,1},{10,2},{11,3},{12,4},{13,5},{14,6},{15,7},{24,16},{25,... | collective-permute-start | bytes 983048 | tf_op jit(solution)/shard_map/ppermute | solution.py:209
  76.1 18.3 %collective-permute-start.8 = (bf16[10,128,128]{2,1,0:T(8,128)(2,1)S(1)}, bf16[10,128,128]{2,1,0:T(8,128)(2,1)S(1)}, u32[]{:S(2)}, u32[]{:S(2)}) collective-permute-start(bf16[10,128,128]{2,1,0:T(8,128)(2,1)S(1)} %get-tuple-element.88), channel_id=1, source_target_pairs={{4,0},{5,1},{6,2},{7,3},{8,4},{9,5},{10,6},{11,7},{12,8},{13,9},{1... | collective-permute-start | bytes 983048 | tf_op jit(solution)/shard_map/ppermute | solution.py:209
  87.3 1.2 copy-start.10
  88.5 1.1 copy-start.12
  92.3 7.6 %copy-start.7 = (f32[384,384]{1,0:T(8,128)S(1)}, f32[384,384]{1,0:T(8,128)}, u32[]{:S(2)}) copy-start(f32[384,384]{1,0:T(8,128)} %fusion.8.mask_ref) | copy-start | bytes 1769476
  92.4 3.9 %collective-permute-start.7 = (f32[6,128,128]{2,1,0:T(8,128)S(1)}, f32[6,128,128]{2,1,0:T(8,128)S(1)}, u32[]{:S(2)}, u32[]{:S(2)}) collective-permute-start(f32[6,128,128]{2,1,0:T(8,128)S(1)} %pad_maximum_fusion.3), channel_id=1, source_target_pairs={{0,1},{1,0},{2,3},{3,2},{4,5},{5,4},{6,7},{7,6},{8,9},{9,8},{10,11... | collective-permute-start | bytes 1179656 | tf_op jit(solution)/shard_map/ppermute | solution.py:209
  94.7 10.5 %collective-permute-start.16 = (bf16[10,128,128]{2,1,0:T(8,128)(2,1)S(1)}, bf16[10,128,128]{2,1,0:T(8,128)(2,1)S(1)}, u32[]{:S(2)}, u32[]{:S(2)}) collective-permute-start(bf16[10,128,128]{2,1,0:T(8,128)(2,1)S(1)} %fusion.3), channel_id=1, source_target_pairs={{0,2},{1,3},{2,0},{3,1},{4,6},{5,7},{6,4},{7,5},{8,10},{9,11},{10,... | collective-permute-start | bytes 983048 | tf_op jit(solution)/shard_map/ppermute | solution.py:209
  96.5 10.4 %collective-permute-start.14 = (bf16[6,128,128]{2,1,0:T(8,128)(2,1)S(1)}, bf16[6,128,128]{2,1,0:T(8,128)(2,1)S(1)}, u32[]{:S(2)}, u32[]{:S(2)}) collective-permute-start(bf16[6,128,128]{2,1,0:T(8,128)(2,1)S(1)} %get-tuple-element.86), channel_id=1, source_target_pairs={{8,0},{9,1},{10,2},{11,3},{12,4},{13,5},{14,6},{15,7},{24,16},{25,... | collective-permute-start | bytes 589832 | tf_op jit(solution)/shard_map/ppermute | solution.py:209
  97.8 12.7 %collective-permute-start.13 = (bf16[6,128,128]{2,1,0:T(8,128)(2,1)S(1)}, bf16[6,128,128]{2,1,0:T(8,128)(2,1)S(1)}, u32[]{:S(2)}, u32[]{:S(2)}) collective-permute-start(bf16[6,128,128]{2,1,0:T(8,128)(2,1)S(1)} %get-tuple-element.86), channel_id=1, source_target_pairs={{4,0},{5,1},{6,2},{7,3},{8,4},{9,5},{10,6},{11,7},{12,8},{13,9},{1... | collective-permute-start | bytes 589832 | tf_op jit(solution)/shard_map/ppermute | solution.py:209
  104.6 7.8 %copy-start.8 = (f32[384,1024]{1,0:T(8,128)S(1)}, f32[384,1024]{1,0:T(8,128)}, u32[]{:S(2)}) copy-start(f32[384,1024]{1,0:T(8,128)} %get-tuple-element.66.ki_ref) | copy-start | bytes 4718596
  104.6 7.8 %copy-start.9 = (f32[384,1024]{1,0:T(8,128)S(1)}, f32[384,1024]{1,0:T(8,128)}, u32[]{:S(2)}) copy-start(f32[384,1024]{1,0:T(8,128)} %get-tuple-element.67.vi_ref) | copy-start | bytes 4718596
  105.6 6.8 %collective-permute-start.17 = (bf16[10,128,128]{2,1,0:T(8,128)(2,1)S(1)}, bf16[10,128,128]{2,1,0:T(8,128)(2,1)S(1)}, u32[]{:S(2)}, u32[]{:S(2)}) collective-permute-start(bf16[10,128,128]{2,1,0:T(8,128)(2,1)S(1)} %get-tuple-element.90), channel_id=1, source_target_pairs={{0,1},{1,0},{2,3},{3,2},{4,5},{5,4},{6,7},{7,6},{8,9},{9,8},{10,11... | collective-permute-start | bytes 983048 | tf_op jit(solution)/shard_map/ppermute | solution.py:209
  110.7 7.3 %collective-permute-start.15 = (bf16[6,128,128]{2,1,0:T(8,128)(2,1)S(1)}, bf16[6,128,128]{2,1,0:T(8,128)(2,1)S(1)}, u32[]{:S(2)}, u32[]{:S(2)}) collective-permute-start(bf16[6,128,128]{2,1,0:T(8,128)(2,1)S(1)} %fusion.13), channel_id=1, source_target_pairs={{0,2},{1,3},{2,0},{3,1},{4,6},{5,7},{6,4},{7,5},{8,10},{9,11},{10,... | collective-permute-start | bytes 589832 | tf_op jit(solution)/shard_map/ppermute | solution.py:209
  118.3 6.0 %collective-permute-start.18 = (bf16[6,128,128]{2,1,0:T(8,128)(2,1)S(1)}, bf16[6,128,128]{2,1,0:T(8,128)(2,1)S(1)}, u32[]{:S(2)}, u32[]{:S(2)}) collective-permute-start(bf16[6,128,128]{2,1,0:T(8,128)(2,1)S(1)} %get-tuple-element.92), channel_id=1, source_target_pairs={{0,1},{1,0},{2,3},{3,2},{4,5},{5,4},{6,7},{7,6},{8,9},{9,8},{10,11... | collective-permute-start | bytes 589832 | tf_op jit(solution)/shard_map/ppermute | solution.py:209
  119.9 4.4 %copy-start.11 = (f32[384,1024]{1,0:T(8,128)S(1)}, f32[384,1024]{1,0:T(8,128)}, u32[]{:S(2)}) copy-start(f32[384,1024]{1,0:T(8,128)} %copy-done.10) | copy-start | bytes 4718596
  119.9 4.4 %copy-start.13 = (f32[384,1024]{1,0:T(8,128)S(1)}, f32[384,1024]{1,0:T(8,128)}, u32[]{:S(2)}) copy-start(f32[384,1024]{1,0:T(8,128)} %copy-done.12) | copy-start | bytes 4718596

commit v4 on v3

--- a/solution.py
+++ b/solution.py
@@ -259,7 +259,7 @@
 
     for start, size in list(zip(starts, CHUNKS))[1:]:
         part = lax.slice_in_dim(after(next_grads, running), start * D, (start + size) * D, axis=2)
-        ready = part if len(grads) == 1 else after(part, grads[0])
+        ready = part if len(grads) == 1 else after(part, grads[len(grads) - 2])
         grads.append(lax.ppermute(ready, "pipe", back))
 
     def halves(table, members):

time: 130 us -> 130 us (level)
  starting transfers between devices: 38.2 us -> 41.1 us
  Pallas kernels: 51 us -> 49.4 us
    pallas_call x9, Pallas kernels: 51 us -> 49.4 us  [call(): pl.pallas_call(kernel, out_shape=tuple(out_shapes), grid_spec=pltpu.Prefe...]
    ppermute x3, starting transfers between devices: 0.16 us -> 1.59 us  [on_device(): grads.append(lax.ppermute(ready, 'pipe', back))]
    ppermute x14, starting transfers between devices: 19 us -> 20.4 us  [moved(): return lax.ppermute(value, 'ctx', pairs)]
  transfers between devices with their start and end apart: 19 -> 19, of which waited for: 6 -> 5; matrix products, arithmetic and copies ran while one was open for 12% -> 11% of each run, Pallas kernels for 36% -> 34%
where the time goes in v4:
time: 130 us
  Pallas kernels  49.4 us (38%)
  starting transfers between devices  41.1 us (32%)
  local copies, waits for them, and re-layouts  16 us (12%)
  waiting for transfers between devices  12.6 us (10%)
  other arithmetic  6.12 us (5%)
  between operations  4.24 us (3%)
    pallas_call x9, Pallas kernels, call(): pl.pallas_call(kernel, out_shape=tuple(out_shapes), grid_spec=pltpu.Prefe...  49.4 us
    ppermute x14, starting transfers between devices, moved(): return lax.ppermute(value, 'ctx', pairs)  20.4 us
    ppermute x1, starting transfers between devices, on_device(): lax.ppermute(docs[-1:] + 1, 'ctx', [(i, i + 1) for i in range(ctx - 1)])[0]  14.3 us
    ppermute x14, waiting for transfers between devices, moved(): return lax.ppermute(value, 'ctx', pairs)  9.17 us
    unnamed x30, local copies, waits for them, and re-layouts  6.13 us
    slice x3, local copies, waits for them, and re-layouts, on_device(): lax.slice_in_dim(after(next_grads, running), start * D, (start + size) *...  5.48 us
    ppermute x1, starting transfers between devices, on_device(): grads = [lax.ppermute(opening, 'pipe', back)]  4.75 us
    ppermute x3, waiting for transfers between devices, on_device(): grads.append(lax.ppermute(ready, 'pipe', back))  3.44 us
  transfers between devices with their start and end apart: 19, of which 5 were waited for; matrix products, arithmetic and copies ran while one was open for 11% of the time, Pallas kernels for 34%

profile of v4, /device:TPU:9, one launch (start us, length us, event | category | flops | bytes accessed | tf_op | source)
XLA Modules:
  0.0 129.8 jit_solution(1993275650926816330)
XLA Ops:
  0.6 1.2 slice.62
  1.8 4.8 %collective-permute-start.2 = (bf16[1,384,1024]{2,1,0:T(8,128)(2,1)S(1)}, bf16[1,384,1024]{2,1,0:T(8,128)(2,1)S(1)}, u32[]{:S(2)}, u32[]{:S(2)}) collective-permute-start(bf16[1,384,1024]{2,1,0:T(8,128)(2,1)S(1)} %slice.62), channel_id=1, source_target_pairs={{16,0},{32,16},{48,32},{64,48},{80,64},{96,80},{112,96},{0,112},{1... | collective-permute-start | bytes 2359304 | tf_op jit(solution)/shard_map/ppermute | solution.py:232
  6.6 0.7 reduce
  7.3 0.6 fusion.28
  8.5 14.3 %collective-permute-start.4 = (s32[1]{0:T(128)}, s32[1]{0:T(128)}, u32[]{:S(2)}, u32[]{:S(2)}) collective-permute-start(s32[1]{0:T(128)} %add.106), channel_id=1, source_target_pairs={{0,1},{1,2},{2,3},{3,4},{4,5},{5,6},{6,7},{7,8},{8,9},{9,10},{10,1... | collective-permute-start | bytes 20 | tf_op jit(solution)/shard_map/ppermute | solution.py:234
  22.9 0.3 fusion.5
  23.2 2.4 %slice.64 = bf16[1,384,1536]{2,1,0:T(8,128)(2,1)} slice(bf16[1,384,4096]{2,1,0:T(8,128)(2,1)} %param.10), slice={[0:1], [0:384], [1024:2560]} | slice | bytes 2359296 | tf_op jit(solution)/shard_map/slice | solution.py:261
  25.6 0.2 slice_reduce_fusion
  25.8 1.0 slice.63
  26.8 0.9 fusion.8.mask_ref
  27.8 2.1 %slice.65 = bf16[1,384,1024]{2,1,0:T(8,128)(2,1)} slice(bf16[1,384,4096]{2,1,0:T(8,128)(2,1)} %param.10), slice={[0:1], [0:384], [2560:3584]} | slice | bytes 1572864 | tf_op jit(solution)/shard_map/slice | solution.py:261
  32.6 1.3 %and_select_fusion = (f32[384]{0:T(512)S(1)}, f32[384]{0:T(512)S(1)}) fusion(s32[384]{0:T(512)S(1)} %reduce, s32[]{:T(128)} %bitcast.2, pred[]{:T(512)S(6)} %eq.45, s32[]{:T(128)} %bitcast.4), kind=kLoop, calls=%fused_computation.48 | loop fusion | flops 1920 | bytes 4617 | tf_op jit(solution)/shard_map/jit(_where)/select_n | solution.py:248
  33.9 0.1 exponential_multiply_fusion.1
  34.1 0.8 maximum_maximum_fusion.pack_ref
  34.8 0.1 collective-permute-start.3
  34.9 0.8 copy-done.14
  35.8 9.9 %inner_grads.4 = (bf16[1,384,4096]{2,1,0:T(8,128)(2,1)}, f32[384,1024]{1,0:T(8,128)}, f32[384,1024]{1,0:T(8,128)}, f32[8,128,128]{2,1,0:T(8,128)}) custom-call(s32[1]{0:T(128)} %bitcast.side_ref, bf16[1,384,4096]{2,1,0:T(8,128)(2,1)} %q_ref.9, bf16[1,384,4096]{2,1,0:T(8,128)(2,1)} %k_ref.15, bf16[1,384,4096]{2,1,0:T(8,128)(2,1)} %v_ref.15, ...), custom_call_target="tpu_custom_call" | custom-call | flops 1107296256 | bytes 31457280 | tf_op jit(solution)/shard_map/inner_grads/pallas_call | solution.py:73
  45.6 0.1 collective-permute-start.6
  45.7 1.1 fusion.26
  46.8 1.3 collective-permute-start.11
  48.1 2.1 %collective-permute-start.10 = (f32[32]{0:T(128)S(1)}, f32[32]{0:T(128)S(1)}, u32[]{:S(2)}, u32[]{:S(2)}) collective-permute-start(f32[32]{0:T(128)S(1)} %get-tuple-element.83), channel_id=1, source_target_pairs={{4,0},{5,1},{6,2},{7,3},{8,4},{9,5},{10,6},{11,7},{12,8},{13,9},{1... | collective-permute-start | bytes 392 | tf_op jit(solution)/shard_map/ppermute | solution.py:209
  50.2 0.1 dynamic-slice_bitcast_fusion.6
  50.4 0.1 dynamic-slice_bitcast_fusion.15
  50.5 3.4 %collective-permute-done.g_ref = bf16[1,384,1536]{2,1,0:T(8,128)(2,1)} collective-permute-done((bf16[1,384,1536]{2,1,0:T(8,128)(2,1)}, bf16[1,384,1536]{2,1,0:T(8,128)(2,1)}, u32[]{:S(2)}, u32[]{:S(2)}) %collective-permute-start) | collective-permute-done | bytes 1179680 | tf_op jit(solution)/shard_map/ppermute | solution.py:263
  54.0 1.9 %copy-done.3 = bf16[1,384,4096]{2,1,0:T(8,128)(2,1)S(1)} copy-done((bf16[1,384,4096]{2,1,0:T(8,128)(2,1)S(1)}, bf16[1,384,4096]{2,1,0:T(8,128)(2,1)}, u32[]{:S(2)}) %copy-start.3) | copy-done | bytes 3145752
  55.9 1.1 copy-done.6
  56.9 12.8 %inner_grads.5 = (bf16[1,384,4096]{2,1,0:T(8,128)(2,1)}, f32[384,1536]{1,0:T(8,128)S(1)}, f32[384,1536]{1,0:T(8,128)S(1)}, f32[12,128,128]{2,1,0:T(8,128)S(1)}) custom-call(s32[1]{0:T(128)} %bitcast.side_ref, bf16[1,384,4096]{2,1,0:T(8,128)(2,1)S(1)} %copy-done.3, bf16[1,384,4096]{2,1,0:T(8,128)(2,1)S(1)} %copy-done.1, ...), custom_call_target="tpu_custom_call", output_to_operand_aliasing={{0}: (8, {})} | custom-call | flops 1660944384 | bytes 47185920 | tf_op jit(solution)/shard_map/inner_grads/pallas_call | solution.py:73
  69.9 0.1 collective-permute-start.5
  70.0 0.1 dynamic-slice_bitcast_fusion.16
  70.0 0.1 maximum_bitcast_fusion.1
  70.4 2.5 %collective-permute-start.12 = (f32[3,32]{1,0:T(4,128)S(1)}, f32[3,32]{1,0:T(4,128)S(1)}, u32[]{:S(2)}, u32[]{:S(2)}) collective-permute-start(f32[3,32]{1,0:T(4,128)S(1)} %pad_maximum_fusion.4), channel_id=1, source_target_pairs={{0,2},{1,3},{2,0},{3,1},{4,6},{5,7},{6,4},{7,5},{8,10},{9,11},{10,... | collective-permute-start | bytes 1160 | tf_op jit(solution)/shard_map/ppermute | solution.py:209
  72.9 1.5 %collective-permute-start.1 = (bf16[1,384,512]{2,1,0:T(8,128)(2,1)S(1)}, bf16[1,384,512]{2,1,0:T(8,128)(2,1)S(1)}, u32[]{:S(2)}, u32[]{:S(2)}) collective-permute-start(bf16[1,384,512]{2,1,0:T(8,128)(2,1)S(1)} %slice.63), channel_id=1, source_target_pairs={{16,0},{32,16},{48,32},{64,48},{80,64},{96,80},{112,96},{0,112},{1... | collective-permute-start | bytes 1179656 | tf_op jit(solution)/shard_map/ppermute | solution.py:263
  74.4 0.2 fusion.23
  74.6 1.3 collective-permute-start.9
  75.9 2.1 %collective-permute-start.8 = (bf16[10,128,128]{2,1,0:T(8,128)(2,1)S(1)}, bf16[10,128,128]{2,1,0:T(8,128)(2,1)S(1)}, u32[]{:S(2)}, u32[]{:S(2)}) collective-permute-start(bf16[10,128,128]{2,1,0:T(8,128)(2,1)S(1)} %get-tuple-element.88), channel_id=1, source_target_pairs={{4,0},{5,1},{6,2},{7,3},{8,4},{9,5},{10,6},{11,7},{12,8},{13,9},{1... | collective-permute-start | bytes 983048 | tf_op jit(solution)/shard_map/ppermute | solution.py:209
  78.0 9.1 %inner_grads.6 = (bf16[1,384,4096]{2,1,0:T(8,128)(2,1)}, f32[384,1024]{1,0:T(8,128)S(1)}, f32[384,1024]{1,0:T(8,128)S(1)}, f32[8,128,128]{2,1,0:T(8,128)S(1)}) custom-call(s32[1]{0:T(128)} %bitcast.side_ref, bf16[1,384,4096]{2,1,0:T(8,128)(2,1)S(1)} %copy-done.3, bf16[1,384,4096]{2,1,0:T(8,128)(2,1)S(1)} %copy-done.1, ...), custom_call_target="tpu_custom_call", output_to_operand_aliasing={{0}: (8, {})} | custom-call | flops 1107296256 | bytes 31457280 | tf_op jit(solution)/shard_map/inner_grads/pallas_call | solution.py:73
  87.1 1.2 copy-done.10
  88.3 1.1 copy-done.12
  89.4 0.1 dynamic-slice_bitcast_fusion.4
  89.8 0.1 dynamic-slice_bitcast_fusion.1
  90.0 0.1 dynamic-slice_bitcast_fusion.11
  90.1 1.2 head_states.1
  91.3 1.4 %collective-permute-start.7 = (f32[6,128,128]{2,1,0:T(8,128)S(1)}, f32[6,128,128]{2,1,0:T(8,128)S(1)}, u32[]{:S(2)}, u32[]{:S(2)}) collective-permute-start(f32[6,128,128]{2,1,0:T(8,128)S(1)} %pad_maximum_fusion.3), channel_id=1, source_target_pairs={{0,1},{1,0},{2,3},{3,2},{4,5},{5,4},{6,7},{7,6},{8,9},{9,8},{10,11... | collective-permute-start | bytes 1179656 | tf_op jit(solution)/shard_map/ppermute | solution.py:209
  93.0 0.1 maximum_bitcast_fusion.7
  93.0 1.6 %collective-permute-done.8 = bf16[10,128,128]{2,1,0:T(8,128)(2,1)S(1)} collective-permute-done((bf16[10,128,128]{2,1,0:T(8,128)(2,1)S(1)}, bf16[10,128,128]{2,1,0:T(8,128)(2,1)S(1)}, u32[]{:S(2)}, u32[]{:S(2)}) %collective-permute-start.8) | collective-permute-done | bytes 327712 | tf_op jit(solution)/shard_map/ppermute | solution.py:209
  94.7 0.3 fusion.3
  94.9 1.8 %collective-permute-start.16 = (bf16[10,128,128]{2,1,0:T(8,128)(2,1)S(1)}, bf16[10,128,128]{2,1,0:T(8,128)(2,1)S(1)}, u32[]{:S(2)}, u32[]{:S(2)}) collective-permute-start(bf16[10,128,128]{2,1,0:T(8,128)(2,1)S(1)} %fusion.3), channel_id=1, source_target_pairs={{0,2},{1,3},{2,0},{3,1},{4,6},{5,7},{6,4},{7,5},{8,10},{9,11},{10,... | collective-permute-start | bytes 983048 | tf_op jit(solution)/shard_map/ppermute | solution.py:209
  96.8 0.1 fusion.22
  96.9 1.3 collective-permute-start.14
  98.2 2.1 %collective-permute-start.13 = (bf16[6,128,128]{2,1,0:T(8,128)(2,1)S(1)}, bf16[6,128,128]{2,1,0:T(8,128)(2,1)S(1)}, u32[]{:S(2)}, u32[]{:S(2)}) collective-permute-start(bf16[6,128,128]{2,1,0:T(8,128)(2,1)S(1)} %get-tuple-element.86), channel_id=1, source_target_pairs={{4,0},{5,1},{6,2},{7,3},{8,4},{9,5},{10,6},{11,7},{12,8},{13,9},{1... | collective-permute-start | bytes 589832 | tf_op jit(solution)/shard_map/ppermute | solution.py:209
  100.4 4.0 %inner_grads.7 = (bf16[1,384,4096]{2,1,0:T(8,128)(2,1)}, f32[384,512]{1,0:T(8,128)S(1)}, f32[384,512]{1,0:T(8,128)S(1)}) custom-call(s32[1]{0:T(128)} %bitcast.side_ref, bf16[1,384,4096]{2,1,0:T(8,128)(2,1)S(1)} %copy-done.3, bf16[1,384,4096]{2,1,0:T(8,128)(2,1)S(1)} %copy-done.1, ...), custom_call_target="tpu_custom_call", output_to_operand_aliasing={{0}: (8, {})} | custom-call | flops 553648128 | bytes 15728640 | tf_op jit(solution)/shard_map/inner_grads/pallas_call | solution.py:73
  104.3 1.0 collective-permute-done.16
  105.3 0.4 select_convert_fusion
  105.7 1.4 %collective-permute-start.17 = (bf16[10,128,128]{2,1,0:T(8,128)(2,1)S(1)}, bf16[10,128,128]{2,1,0:T(8,128)(2,1)S(1)}, u32[]{:S(2)}, u32[]{:S(2)}) collective-permute-start(bf16[10,128,128]{2,1,0:T(8,128)(2,1)S(1)} %get-tuple-element.90), channel_id=1, source_target_pairs={{0,1},{1,0},{2,3},{3,2},{4,5},{5,4},{6,7},{7,6},{8,9},{9,8},{10,11... | collective-permute-start | bytes 983048 | tf_op jit(solution)/shard_map/ppermute | solution.py:209
  107.1 3.8 %collective-permute-done.13 = bf16[6,128,128]{2,1,0:T(8,128)(2,1)S(1)} collective-permute-done((bf16[6,128,128]{2,1,0:T(8,128)(2,1)S(1)}, bf16[6,128,128]{2,1,0:T(8,128)(2,1)S(1)}, u32[]{:S(2)}, u32[]{:S(2)}) %collective-permute-start.13) | collective-permute-done | bytes 196640 | tf_op jit(solution)/shard_map/ppermute | solution.py:209
  111.0 0.2 fusion.13
  111.1 1.3 %collective-permute-start.15 = (bf16[6,128,128]{2,1,0:T(8,128)(2,1)S(1)}, bf16[6,128,128]{2,1,0:T(8,128)(2,1)S(1)}, u32[]{:S(2)}, u32[]{:S(2)}) collective-permute-start(bf16[6,128,128]{2,1,0:T(8,128)(2,1)S(1)} %fusion.13), channel_id=1, source_target_pairs={{0,2},{1,3},{2,0},{3,1},{4,6},{5,7},{6,4},{7,5},{8,10},{9,11},{10,... | collective-permute-start | bytes 589832 | tf_op jit(solution)/shard_map/ppermute | solution.py:209
  112.6 3.1 %finish_grads.4 = (bf16[1,384,4096]{2,1,0:T(8,128)(2,1)}, bf16[1,384,4096]{2,1,0:T(8,128)(2,1)}) custom-call(s32[1]{0:T(128)} %bitcast.side_ref, bf16[1,384,4096]{2,1,0:T(8,128)(2,1)S(1)} %copy-done.1, bf16[1,384,4096]{2,1,0:T(8,128)(2,1)S(1)} %copy-done.2, f32[384,1024]{1,0:T(8,128)S(1)} %copy-done.8, f32[384,1024]{1,0:T(8,128)S(1)} %copy-done.9, ...), custom_call_target="tpu_custom_call" | custom-call | flops 201326592 | bytes 11796480 | tf_op jit(solution)/shard_map/finish_grads/pallas_call | solution.py:73
  115.8 2.7 %collective-permute-done.15 = bf16[6,128,128]{2,1,0:T(8,128)(2,1)S(1)} collective-permute-done((bf16[6,128,128]{2,1,0:T(8,128)(2,1)S(1)}, bf16[6,128,128]{2,1,0:T(8,128)(2,1)S(1)}, u32[]{:S(2)}, u32[]{:S(2)}) %collective-permute-start.15) | collective-permute-done | bytes 196640 | tf_op jit(solution)/shard_map/ppermute | solution.py:209
  118.5 0.3 select_convert_fusion.2
  118.7 1.7 %collective-permute-start.18 = (bf16[6,128,128]{2,1,0:T(8,128)(2,1)S(1)}, bf16[6,128,128]{2,1,0:T(8,128)(2,1)S(1)}, u32[]{:S(2)}, u32[]{:S(2)}) collective-permute-start(bf16[6,128,128]{2,1,0:T(8,128)(2,1)S(1)} %get-tuple-element.92), channel_id=1, source_target_pairs={{0,1},{1,0},{2,3},{3,2},{4,5},{5,4},{6,7},{7,6},{8,9},{9,8},{10,11... | collective-permute-start | bytes 589832 | tf_op jit(solution)/shard_map/ppermute | solution.py:209
  120.4 4.4 %finish_grads.5 = (bf16[1,384,4096]{2,1,0:T(8,128)(2,1)}, bf16[1,384,4096]{2,1,0:T(8,128)(2,1)}) custom-call(s32[1]{0:T(128)} %bitcast.side_ref, bf16[1,384,4096]{2,1,0:T(8,128)(2,1)S(1)} %copy-done.1, bf16[1,384,4096]{2,1,0:T(8,128)(2,1)S(1)} %copy-done.2, f32[384,1536]{1,0:T(8,128)S(1)} %get-tuple-element.75.ki_ref, ...), custom_call_target="tpu_custom_call", output_to_operand_aliasing={{0}: (8, {}), {1}: (9, {})} | custom-call | flops 301989888 | bytes 17694720 | tf_op jit(solution)/shard_map/finish_grads/pallas_call | solution.py:73
  124.8 3.2 %finish_grads.6 = (bf16[1,384,4096]{2,1,0:T(8,128)(2,1)}, bf16[1,384,4096]{2,1,0:T(8,128)(2,1)}) custom-call(s32[1]{0:T(128)} %bitcast.side_ref, bf16[1,384,4096]{2,1,0:T(8,128)(2,1)S(1)} %copy-done.1, bf16[1,384,4096]{2,1,0:T(8,128)(2,1)S(1)} %copy-done.2, f32[384,1024]{1,0:T(8,128)S(1)} %copy-done.11, ...), custom_call_target="tpu_custom_call", output_to_operand_aliasing={{0}: (8, {}), {1}: (9, {})} | custom-call | flops 201326592 | bytes 11796480 | tf_op jit(solution)/shard_map/finish_grads/pallas_call | solution.py:73
  128.0 1.8 %finish_grads.7 = (bf16[1,384,4096]{2,1,0:T(8,128)(2,1)}, bf16[1,384,4096]{2,1,0:T(8,128)(2,1)}) custom-call(s32[1]{0:T(128)} %bitcast.side_ref, bf16[1,384,4096]{2,1,0:T(8,128)(2,1)S(1)} %copy-done.1, bf16[1,384,4096]{2,1,0:T(8,128)(2,1)S(1)} %copy-done.2, f32[384,512]{1,0:T(8,128)S(1)} %get-tuple-element.62.ki_ref, ...), custom_call_target="tpu_custom_call", output_to_operand_aliasing={{0}: (8, {}), {1}: (9, {})} | custom-call | flops 100663296 | bytes 5898240 | tf_op jit(solution)/shard_map/finish_grads/pallas_call | solution.py:73
  (71 shorter events, 1.7 us)
Async XLA Ops:
  0.6 22.2 %copy-start = (f32[1,32,384]{2,1,0:T(8,128)S(1)}, f32[1,32,384]{2,1,0:T(8,128)}, u32[]{:S(2)}) copy-start(f32[1,32,384]{2,1,0:T(8,128)} %param.11) | copy-start | bytes 147460
  1.8 33.0 %collective-permute-start.2 = (bf16[1,384,1024]{2,1,0:T(8,128)(2,1)S(1)}, bf16[1,384,1024]{2,1,0:T(8,128)(2,1)S(1)}, u32[]{:S(2)}, u32[]{:S(2)}) collective-permute-start(bf16[1,384,1024]{2,1,0:T(8,128)(2,1)S(1)} %slice.62), channel_id=1, source_target_pairs={{16,0},{32,16},{48,32},{64,48},{80,64},{96,80},{112,96},{0,112},{1... | collective-permute-start | bytes 2359304 | tf_op jit(solution)/shard_map/ppermute | solution.py:232
  8.5 23.4 %collective-permute-start.4 = (s32[1]{0:T(128)}, s32[1]{0:T(128)}, u32[]{:S(2)}, u32[]{:S(2)}) collective-permute-start(s32[1]{0:T(128)} %add.106), channel_id=1, source_target_pairs={{0,1},{1,2},{2,3},{3,4},{4,5},{5,6},{6,7},{7,8},{8,9},{9,10},{10,1... | collective-permute-start | bytes 20 | tf_op jit(solution)/shard_map/ppermute | solution.py:234
  25.6 28.4 %collective-permute-start = (bf16[1,384,1536]{2,1,0:T(8,128)(2,1)}, bf16[1,384,1536]{2,1,0:T(8,128)(2,1)}, u32[]{:S(2)}, u32[]{:S(2)}) collective-permute-start(bf16[1,384,1536]{2,1,0:T(8,128)(2,1)} %slice.64), channel_id=1, source_target_pairs={{16,0},{32,16},{48,32},{64,48},{80,64},{96,80},{112,96},{0,112},{1... | collective-permute-start | bytes 3538952 | tf_op jit(solution)/shard_map/ppermute | solution.py:263
  34.8 0.9 copy-start.14
  34.8 39.6 %collective-permute-start.3 = (bf16[1,384,1024]{2,1,0:T(8,128)(2,1)}, bf16[1,384,1024]{2,1,0:T(8,128)(2,1)}, u32[]{:S(2)}, u32[]{:S(2)}) collective-permute-start(bf16[1,384,1024]{2,1,0:T(8,128)(2,1)} %slice.65), channel_id=1, source_target_pairs={{16,0},{32,16},{48,32},{64,48},{80,64},{96,80},{112,96},{0,112},{1... | collective-permute-start | bytes 2359304 | tf_op jit(solution)/shard_map/ppermute | solution.py:263
  35.8 18.2 %copy-start.1 = (bf16[1,384,4096]{2,1,0:T(8,128)(2,1)S(1)}, bf16[1,384,4096]{2,1,0:T(8,128)(2,1)}, u32[]{:S(2)}) copy-start(bf16[1,384,4096]{2,1,0:T(8,128)(2,1)} %k_ref.15) | copy-start | bytes 9437188
  35.8 18.2 %copy-start.4 = (f32[1,1,32,128,128]{4,3,2,1,0:T(8,128)S(1)}, f32[1,1,32,128,128]{4,3,2,1,0:T(8,128)}, u32[]{:S(2)}) copy-start(f32[1,1,32,128,128]{4,3,2,1,0:T(8,128)} %p_ref.7) | copy-start | bytes 6291460
  35.8 18.2 %copy-start.5 = (f32[16,8,384]{2,1,0:T(8,128)S(1)}, f32[16,8,384]{2,1,0:T(8,128)}, u32[]{:S(2)}) copy-start(f32[16,8,384]{2,1,0:T(8,128)} %maximum_maximum_fusion.pack_ref) | copy-start | bytes 589828
  45.6 1.2 collective-permute-start.6
  46.8 23.5 %collective-permute-start.11 = (f32[32]{0:T(128)S(1)}, f32[32]{0:T(128)S(1)}, u32[]{:S(2)}, u32[]{:S(2)}) collective-permute-start(f32[32]{0:T(128)S(1)} %get-tuple-element.83), channel_id=1, source_target_pairs={{8,0},{9,1},{10,2},{11,3},{12,4},{13,5},{14,6},{15,7},{24,16},{25,... | collective-permute-start | bytes 392 | tf_op jit(solution)/shard_map/ppermute | solution.py:209
  48.1 22.2 %collective-permute-start.10 = (f32[32]{0:T(128)S(1)}, f32[32]{0:T(128)S(1)}, u32[]{:S(2)}, u32[]{:S(2)}) collective-permute-start(f32[32]{0:T(128)S(1)} %get-tuple-element.83), channel_id=1, source_target_pairs={{4,0},{5,1},{6,2},{7,3},{8,4},{9,5},{10,6},{11,7},{12,8},{13,9},{1... | collective-permute-start | bytes 392 | tf_op jit(solution)/shard_map/ppermute | solution.py:209
  54.0 1.9 %copy-start.3 = (bf16[1,384,4096]{2,1,0:T(8,128)(2,1)S(1)}, bf16[1,384,4096]{2,1,0:T(8,128)(2,1)}, u32[]{:S(2)}) copy-start(bf16[1,384,4096]{2,1,0:T(8,128)(2,1)} %q_ref.9) | copy-start | bytes 9437188
  55.9 1.1 copy-start.6
  69.8 8.2 %copy-start.2 = (bf16[1,384,4096]{2,1,0:T(8,128)(2,1)S(1)}, bf16[1,384,4096]{2,1,0:T(8,128)(2,1)}, u32[]{:S(2)}) copy-start(bf16[1,384,4096]{2,1,0:T(8,128)(2,1)} %v_ref.15) | copy-start | bytes 9437188
  69.9 4.5 %collective-permute-start.5 = (f32[10,128,128]{2,1,0:T(8,128)S(1)}, f32[10,128,128]{2,1,0:T(8,128)S(1)}, u32[]{:S(2)}, u32[]{:S(2)}) collective-permute-start(f32[10,128,128]{2,1,0:T(8,128)S(1)} %pad_maximum_fusion.1), channel_id=1, source_target_pairs={{0,1},{1,0},{2,3},{3,2},{4,5},{5,4},{6,7},{7,6},{8,9},{9,8},{10,11... | collective-permute-start | bytes 1966088 | tf_op jit(solution)/shard_map/ppermute | solution.py:209
  70.4 19.0 %collective-permute-start.12 = (f32[3,32]{1,0:T(4,128)S(1)}, f32[3,32]{1,0:T(4,128)S(1)}, u32[]{:S(2)}, u32[]{:S(2)}) collective-permute-start(f32[3,32]{1,0:T(4,128)S(1)} %pad_maximum_fusion.4), channel_id=1, source_target_pairs={{0,2},{1,3},{2,0},{3,1},{4,6},{5,7},{6,4},{7,5},{8,10},{9,11},{10,... | collective-permute-start | bytes 1160 | tf_op jit(solution)/shard_map/ppermute | solution.py:209
  72.9 17.2 %collective-permute-start.1 = (bf16[1,384,512]{2,1,0:T(8,128)(2,1)S(1)}, bf16[1,384,512]{2,1,0:T(8,128)(2,1)S(1)}, u32[]{:S(2)}, u32[]{:S(2)}) collective-permute-start(bf16[1,384,512]{2,1,0:T(8,128)(2,1)S(1)} %slice.63), channel_id=1, source_target_pairs={{16,0},{32,16},{48,32},{64,48},{80,64},{96,80},{112,96},{0,112},{1... | collective-permute-start | bytes 1179656 | tf_op jit(solution)/shard_map/ppermute | solution.py:263
  74.6 18.4 %collective-permute-start.9 = (bf16[10,128,128]{2,1,0:T(8,128)(2,1)S(1)}, bf16[10,128,128]{2,1,0:T(8,128)(2,1)S(1)}, u32[]{:S(2)}, u32[]{:S(2)}) collective-permute-start(bf16[10,128,128]{2,1,0:T(8,128)(2,1)S(1)} %get-tuple-element.88), channel_id=1, source_target_pairs={{8,0},{9,1},{10,2},{11,3},{12,4},{13,5},{14,6},{15,7},{24,16},{25,... | collective-permute-start | bytes 983048 | tf_op jit(solution)/shard_map/ppermute | solution.py:209
  75.9 18.8 %collective-permute-start.8 = (bf16[10,128,128]{2,1,0:T(8,128)(2,1)S(1)}, bf16[10,128,128]{2,1,0:T(8,128)(2,1)S(1)}, u32[]{:S(2)}, u32[]{:S(2)}) collective-permute-start(bf16[10,128,128]{2,1,0:T(8,128)(2,1)S(1)} %get-tuple-element.88), channel_id=1, source_target_pairs={{4,0},{5,1},{6,2},{7,3},{8,4},{9,5},{10,6},{11,7},{12,8},{13,9},{1... | collective-permute-start | bytes 983048 | tf_op jit(solution)/shard_map/ppermute | solution.py:209
  87.1 1.2 copy-start.10
  88.3 1.1 copy-start.12
  91.2 9.1 %copy-start.7 = (f32[384,384]{1,0:T(8,128)S(1)}, f32[384,384]{1,0:T(8,128)}, u32[]{:S(2)}) copy-start(f32[384,384]{1,0:T(8,128)} %fusion.8.mask_ref) | copy-start | bytes 1769476
  91.3 5.5 %collective-permute-start.7 = (f32[6,128,128]{2,1,0:T(8,128)S(1)}, f32[6,128,128]{2,1,0:T(8,128)S(1)}, u32[]{:S(2)}, u32[]{:S(2)}) collective-permute-start(f32[6,128,128]{2,1,0:T(8,128)S(1)} %pad_maximum_fusion.3), channel_id=1, source_target_pairs={{0,1},{1,0},{2,3},{3,2},{4,5},{5,4},{6,7},{7,6},{8,9},{9,8},{10,11... | collective-permute-start | bytes 1179656 | tf_op jit(solution)/shard_map/ppermute | solution.py:209
  94.9 10.4 %collective-permute-start.16 = (bf16[10,128,128]{2,1,0:T(8,128)(2,1)S(1)}, bf16[10,128,128]{2,1,0:T(8,128)(2,1)S(1)}, u32[]{:S(2)}, u32[]{:S(2)}) collective-permute-start(bf16[10,128,128]{2,1,0:T(8,128)(2,1)S(1)} %fusion.3), channel_id=1, source_target_pairs={{0,2},{1,3},{2,0},{3,1},{4,6},{5,7},{6,4},{7,5},{8,10},{9,11},{10,... | collective-permute-start | bytes 983048 | tf_op jit(solution)/shard_map/ppermute | solution.py:209
  96.9 10.2 %collective-permute-start.14 = (bf16[6,128,128]{2,1,0:T(8,128)(2,1)S(1)}, bf16[6,128,128]{2,1,0:T(8,128)(2,1)S(1)}, u32[]{:S(2)}, u32[]{:S(2)}) collective-permute-start(bf16[6,128,128]{2,1,0:T(8,128)(2,1)S(1)} %get-tuple-element.86), channel_id=1, source_target_pairs={{8,0},{9,1},{10,2},{11,3},{12,4},{13,5},{14,6},{15,7},{24,16},{25,... | collective-permute-start | bytes 589832 | tf_op jit(solution)/shard_map/ppermute | solution.py:209
  98.2 12.7 %collective-permute-start.13 = (bf16[6,128,128]{2,1,0:T(8,128)(2,1)S(1)}, bf16[6,128,128]{2,1,0:T(8,128)(2,1)S(1)}, u32[]{:S(2)}, u32[]{:S(2)}) collective-permute-start(bf16[6,128,128]{2,1,0:T(8,128)(2,1)S(1)} %get-tuple-element.86), channel_id=1, source_target_pairs={{4,0},{5,1},{6,2},{7,3},{8,4},{9,5},{10,6},{11,7},{12,8},{13,9},{1... | collective-permute-start | bytes 589832 | tf_op jit(solution)/shard_map/ppermute | solution.py:209
  104.3 8.3 %copy-start.8 = (f32[384,1024]{1,0:T(8,128)S(1)}, f32[384,1024]{1,0:T(8,128)}, u32[]{:S(2)}) copy-start(f32[384,1024]{1,0:T(8,128)} %get-tuple-element.66.ki_ref) | copy-start | bytes 4718596
  104.3 8.3 %copy-start.9 = (f32[384,1024]{1,0:T(8,128)S(1)}, f32[384,1024]{1,0:T(8,128)}, u32[]{:S(2)}) copy-start(f32[384,1024]{1,0:T(8,128)} %get-tuple-element.67.vi_ref) | copy-start | bytes 4718596
  105.7 6.9 %collective-permute-start.17 = (bf16[10,128,128]{2,1,0:T(8,128)(2,1)S(1)}, bf16[10,128,128]{2,1,0:T(8,128)(2,1)S(1)}, u32[]{:S(2)}, u32[]{:S(2)}) collective-permute-start(bf16[10,128,128]{2,1,0:T(8,128)(2,1)S(1)} %get-tuple-element.90), channel_id=1, source_target_pairs={{0,1},{1,0},{2,3},{3,2},{4,5},{5,4},{6,7},{7,6},{8,9},{9,8},{10,11... | collective-permute-start | bytes 983048 | tf_op jit(solution)/shard_map/ppermute | solution.py:209
  111.1 7.3 %collective-permute-start.15 = (bf16[6,128,128]{2,1,0:T(8,128)(2,1)S(1)}, bf16[6,128,128]{2,1,0:T(8,128)(2,1)S(1)}, u32[]{:S(2)}, u32[]{:S(2)}) collective-permute-start(bf16[6,128,128]{2,1,0:T(8,128)(2,1)S(1)} %fusion.13), channel_id=1, source_target_pairs={{0,2},{1,3},{2,0},{3,1},{4,6},{5,7},{6,4},{7,5},{8,10},{9,11},{10,... | collective-permute-start | bytes 589832 | tf_op jit(solution)/shard_map/ppermute | solution.py:209
  118.7 6.0 %collective-permute-start.18 = (bf16[6,128,128]{2,1,0:T(8,128)(2,1)S(1)}, bf16[6,128,128]{2,1,0:T(8,128)(2,1)S(1)}, u32[]{:S(2)}, u32[]{:S(2)}) collective-permute-start(bf16[6,128,128]{2,1,0:T(8,128)(2,1)S(1)} %get-tuple-element.92), channel_id=1, source_target_pairs={{0,1},{1,0},{2,3},{3,2},{4,5},{5,4},{6,7},{7,6},{8,9},{9,8},{10,11... | collective-permute-start | bytes 589832 | tf_op jit(solution)/shard_map/ppermute | solution.py:209
  120.4 4.4 %copy-start.11 = (f32[384,1024]{1,0:T(8,128)S(1)}, f32[384,1024]{1,0:T(8,128)}, u32[]{:S(2)}) copy-start(f32[384,1024]{1,0:T(8,128)} %copy-done.10) | copy-start | bytes 4718596
  120.4 4.4 %copy-start.13 = (f32[384,1024]{1,0:T(8,128)S(1)}, f32[384,1024]{1,0:T(8,128)}, u32[]{:S(2)}) copy-start(f32[384,1024]{1,0:T(8,128)} %copy-done.12) | copy-start | bytes 4718596
